TPU v7x, 128 devices: a whole 4x4x4 slice. The times are simulated.
128 devices in a mesh: tok: 8 (over y, core), exp: 16 (over x, z).
Axes of the slice: x: 4, y: 4, z: 4, core: 2. Of those that a mesh axis runs over, the one named last changes fastest.
Arguments:
- tokens: bfloat16 [8192, 4096], P(('tok', 'exp')), may hold values from -6 to 6
- cotangent: bfloat16 [8192, 4096], P(('tok', 'exp')), may hold values from -6 to 6
- expert_ids: int32 [8192, 8], P(('tok', 'exp')), may hold values from 0 to 127, as said below
- gate_weights: bfloat16 [8192, 8], P(('tok', 'exp')), may hold values from 0.099609375 to 1
- w_in: bfloat16 [16, 2, 1536, 4096], P('exp', None, 'tok'), may hold values from -0.09375 to 0.09375
- w_down: bfloat16 [16, 1536, 4096], P('exp', 'tok'), may hold values from -0.3125 to 0.3125
Outputs:
- moe_out: bfloat16 [8192, 4096], P(('tok', 'exp'))
- token_grad: bfloat16 [8192, 4096], P(('tok', 'exp'))
- grad_w_in: bfloat16 [16, 2, 1536, 4096], P('exp', None, 'tok')
- grad_w_down: bfloat16 [16, 1536, 4096], P('exp', 'tok')
Inputs may be any that keep to these rules, and one draw needn't show every extreme that they name: `expert_ids`: each row names 8 different experts. Among the 64 rows of one device no expert below 16 is named by more than 2 rows, and one expert below 16, the same on every device, is named by exactly 2 rows of every device.
All inputs are finite; a program needn't handle non-finite values.
Results may differ from a plain program's by a relative error of at most 0.0058.
Values may be sent and summed in bfloat16 or wider, within the bound.
A program may use at most 128 MiB of HBM per device.

v0:
```python
import jax
import jax.numpy as jnp
from jax import lax
from jax.sharding import PartitionSpec as P

CAP = 2


def in_one_piece(arrays, axis, split_dim, concat_dim, along):
    both = jnp.concatenate(arrays, axis=along)
    result, at, gathered = (
        lax.all_to_all(both, axis, split_axis=split_dim, concat_axis=concat_dim, tiled=True),
        0,
        [],
    )
    for a in arrays:
        gathered.append(lax.slice_in_dim(result, at, at + a.shape[along], axis=along))
        at += a.shape[along]
    return tuple(gathered)


def in_one_piece_2(arrays, axis, dim, along):
    ends, at = ([], 0)
    for a in arrays[:-1]:
        at += a.shape[along]
        ends.append(at)
    both = jnp.concatenate(arrays, axis=along)
    return tuple(jnp.split(lax.all_gather(both, axis, axis=dim, tiled=True), ends, axis=along))


def in_one_piece_3(arrays, axis, dim, along):
    ends, at = ([], 0)
    for a in arrays[:-1]:
        at += a.shape[along]
        ends.append(at)
    both = jnp.concatenate(arrays, axis=along)
    return tuple(
        jnp.split(lax.psum_scatter(both, axis, scatter_dimension=dim, tiled=True), ends, axis=along)
    )


def build_tables(expert_ids, gate_weights, experts, capacity):
    count_rows, count_top = expert_ids.shape
    flat_ids = expert_ids.reshape(count_rows * count_top)
    owners = jnp.arange(experts, dtype=jnp.int32)
    onehot = (flat_ids[:, None] == owners[None, :]).astype(jnp.int32)
    before = jnp.cumsum(onehot, axis=0) - onehot
    slots = jnp.sum(before * onehot, axis=1)
    target = jnp.where(flat_ids < experts, flat_ids * capacity + slots, experts * capacity)
    place_table = jnp.arange(experts * capacity, dtype=jnp.int32)
    matches = (place_table[:, None] == target[None, :]).reshape(
        experts * capacity, count_rows, count_top
    )
    picked = jnp.sum(matches.astype(jnp.float32), axis=2).astype(jnp.bfloat16)
    weighted = jnp.sum(
        jnp.where(matches, gate_weights.astype(jnp.float32)[None, :, :], 0.0), axis=2
    )
    return (picked, weighted.astype(jnp.bfloat16))


def expert_slice(routed, routed_cot, weight_in, weight_down):
    gate_act = jnp.einsum("rd,fd->rf", routed, weight_in[0], preferred_element_type=jnp.float32)
    up_act = jnp.einsum("rd,fd->rf", routed, weight_in[1], preferred_element_type=jnp.float32)
    sigmoid_gate = jax.nn.sigmoid(gate_act)
    silu_gate = gate_act * sigmoid_gate
    hidden = (silu_gate * up_act).astype(jnp.bfloat16)
    out_part = jnp.dot(hidden, weight_down, preferred_element_type=jnp.float32)
    hidden_grad = jnp.einsum(
        "rd,fd->rf", routed_cot, weight_down, preferred_element_type=jnp.float32
    )
    gate_grad = (
        hidden_grad * up_act * sigmoid_gate * (1.0 + gate_act * (1.0 - sigmoid_gate))
    ).astype(jnp.bfloat16)
    up_grad = (hidden_grad * silu_gate).astype(jnp.bfloat16)
    grad_part = jnp.dot(gate_grad, weight_in[0], preferred_element_type=jnp.float32) + jnp.dot(
        up_grad, weight_in[1], preferred_element_type=jnp.float32
    )
    grad_gate = jnp.einsum("rf,rd->fd", gate_grad, routed, preferred_element_type=jnp.float32)
    grad_up = jnp.einsum("rf,rd->fd", up_grad, routed, preferred_element_type=jnp.float32)
    grad_down = jnp.einsum("rf,rd->fd", hidden, routed_cot, preferred_element_type=jnp.float32)
    grad_in = jnp.stack([grad_gate, grad_up]).astype(jnp.bfloat16)
    return (out_part, grad_part, grad_in, grad_down.astype(jnp.bfloat16))


def body(tokens, cotangent, expert_ids, gate_weights, w_in, w_down):
    experts = lax.axis_size("exp")
    picked, weighted = build_tables(expert_ids, gate_weights, experts, CAP)
    send_rows = jnp.dot(picked, tokens, preferred_element_type=jnp.float32).astype(jnp.bfloat16)
    send_cot = jnp.dot(weighted, cotangent, preferred_element_type=jnp.float32).astype(jnp.bfloat16)
    near_rows, near_cot = in_one_piece((send_rows, send_cot), "exp", 0, 0, 1)
    routed, routed_cot = in_one_piece_2((near_rows, near_cot), "tok", 0, 1)
    out_part, grad_part, grad_in, grad_down = expert_slice(routed, routed_cot, w_in[0], w_down[0])
    summed_out, summed_grad = in_one_piece_3((out_part, grad_part), "tok", 0, 1)
    out_rows, grad_rows = in_one_piece(
        (summed_out.astype(jnp.bfloat16), summed_grad.astype(jnp.bfloat16)), "exp", 0, 0, 1
    )
    moe_out = jnp.dot(weighted.T, out_rows, preferred_element_type=jnp.float32).astype(jnp.bfloat16)
    token_grad = jnp.dot(picked.T, grad_rows, preferred_element_type=jnp.float32).astype(
        jnp.bfloat16
    )
    return (moe_out, token_grad, grad_in[None], grad_down[None])


def solution(mesh):
    placed = (
        P(("tok", "exp"), None),
        P(("tok", "exp"), None),
        P(("tok", "exp"), None),
        P(("tok", "exp"), None),
        P("exp", None, "tok", None),
        P("exp", "tok", None),
    )
    return jax.shard_map(
        body,
        mesh=mesh,
        in_specs=placed,
        out_specs=(
            P(("tok", "exp"), None),
            P(("tok", "exp"), None),
            P("exp", None, "tok", None),
            P("exp", "tok", None),
        ),
        check_vma=False,
    )
```

profile of v0, /device:TPU:0, one launch (start us, length us, event | category | flops | bytes accessed | tf_op | source)
XLA Modules:
  0.0 162.1 jit_solution(13749186091471365226)
XLA Ops:
  7.2 0.0 copy-start
  7.2 0.0 all-gather.2.cloned.1.call-start
  7.2 0.9 copy.28
  8.1 0.1 eq.44
  8.2 0.1 eq.40
  8.3 1.2 reduce-window.6
  9.5 0.2 slice_reduce_fusion
  9.7 0.1 fusion.29
  9.8 0.1 reduce_sum.30
  9.9 0.1 copy.31
  10.0 0.7 add_select_fusion
  10.7 0.7 convert_element_type.55
  11.4 0.1 convert_reduce_fusion
  11.5 1.3 convolution_convert_fusion.5
  12.7 1.3 convolution_convert_fusion.6
  14.0 0.3 all_to_all.16
  14.4 19.3 %all_to_all.24 = bf16[16,2,8192]{2,1,0:T(2,128)(2,1)S(1)} all-to-all(bf16[16,2,8192]{2,1,0:T(2,128)(2,1)S(1)} %all_to_all.16), channel_id=1, replica_groups=mesh['tok'=8,'exp'=16] {'exp'}, dimensions={0} | all-to-all | bytes 1048576 | tf_op jit(solution)/shard_map/all_to_all | solution.py:12
  33.6 1.0 all_to_all.18
  34.6 0.0 all-gather.2.cloned.1.call-update
  34.7 0.0 reduce-scatter.2.cloned.1.call-start
  34.7 30.2 %all-gather.2.cloned.1.call-done = bf16[256,8192]{1,0:T(8,128)(2,1)} async-done(((bf16[32,8192]{1,0:T(8,128)(2,1)}), bf16[256,8192]{1,0:T(8,128)(2,1)}) %all-gather.2.cloned.1.call-update) | async-done | bytes 4194320 | tf_op jit(solution)/shard_map/all_gather | solution.py:28
  64.9 0.0 copy-start.1
  64.9 3.0 %fusion.14 = f32[256,192]{0,1:T(8,128)S(1)} fusion(bf16[1,2,192,4096]{3,2,1,0:T(8,128)(2,1)} %param.10, bf16[256,8192]{1,0:T(8,128)(2,1)} %all-gather.2.cloned.1.call-done), kind=kOutput, calls=%fused_computation.24 | convolution fusion | flops 402653184 | bytes 3866624 | tf_op jit(solution)/shard_map/rd,fd->rf/dot_general | solution.py:62
  67.9 0.0 copy-done
  67.9 0.2 copy-done.1
  68.2 0.0 copy-start.3
  68.2 0.8 fusion.4
  69.0 1.0 copy-done.3
  70.1 0.9 multiply_convert_fusion.2
  70.9 0.7 fusion.12
  71.7 0.7 fusion.7
  72.4 0.7 convolution_add_fusion
  73.1 3.8 %pad_maximum_fusion = f32[256,8192]{1,0:T(8,128)} fusion(f32[256,4096]{1,0:T(8,128)S(1)} %convolution_add_fusion, f32[256,4096]{1,0:T(8,128)S(1)} %fusion.7), kind=kLoop, calls=%fused_computation | loop fusion | flops 2097152 | bytes 16777216 | tf_op jit(solution)/shard_map/concatenate | solution.py:36
  76.9 0.0 reduce-scatter.2.cloned.1.call-update
  77.0 0.0 copy-start.2
  77.0 2.3 %fusion = bf16[1,1,192,4096]{3,2,1,0:T(8,128)(2,1)S(1)} fusion(bf16[256,192]{0,1:T(8,128)(2,1)S(1)} %get-tuple-element.7, bf16[256,8192]{1,0:T(8,128)(2,1)} %all-gather.2.cloned.1.call-done), kind=kOutput, calls=%fused_computation.5 | convolution fusion | flops 403439616 | bytes 3768320 | tf_op jit(solution)/shard_map/rf,rd->fd/dot_general | solution.py:78
  79.3 3.4 %fusion.1 = bf16[1,1,192,4096]{3,2,1,0:T(8,128)(2,1)} fusion(bf16[256,192]{0,1:T(8,128)(2,1)S(1)} %get-tuple-element.8, bf16[256,8192]{1,0:T(8,128)(2,1)} %all-gather.2.cloned.1.call-done), kind=kOutput, calls=%fused_computation.6 | convolution fusion | flops 403439616 | bytes 3768320 | tf_op jit(solution)/shard_map/rf,rd->fd/dot_general | solution.py:79
  82.7 0.0 copy-done.2
  82.7 1.7 %fusion.2 = bf16[1,192,4096]{2,1,0:T(8,128)(2,1)} fusion(bf16[256,192]{0,1:T(8,128)(2,1)S(1)} %get-tuple-element.6, bf16[256,8192]{1,0:T(8,128)(2,1)S(1)} %copy-done.2), kind=kOutput, calls=%fused_computation.7 | convolution fusion | flops 403439616 | bytes 3768320 | tf_op jit(solution)/shard_map/rf,rd->fd/dot_general | solution.py:80
  84.4 45.1 %reduce-scatter.2.cloned.1.call-done = f32[32,8192]{1,0:T(8,128)} async-done(((f32[256,8192]{1,0:T(8,128)}), f32[32,8192]{1,0:T(8,128)}) %reduce-scatter.2.cloned.1.call-update) | async-done | bytes 1048592 | tf_op jit(solution)/shard_map/reduce_scatter | solution.py:38
  129.5 2.1 %convert.12 = bf16[32,8192]{1,0:T(8,128)(2,1)} convert(f32[32,8192]{1,0:T(8,128)} %reduce-scatter.2.cloned.1.call-done) | non-fusion elementwise | flops 262144 | bytes 1572864 | tf_op jit(solution)/shard_map/convert.5
  131.6 2.2 %all_to_all.19 = bf16[16,2,8192]{2,1,0:T(2,128)(2,1)} reshape(bf16[32,8192]{1,0:T(8,128)(2,1)} %convert.12) | data formatting | bytes 1048576 | tf_op jit(solution)/shard_map/all_to_all | solution.py:12
  133.8 7.0 %all-to-all-start.1 = ((bf16[16,2,8192]{2,1,0:T(2,128)(2,1)}), bf16[16,2,8192]{2,1,0:T(2,128)(2,1)}, u32[]{:S(2)}, u32[]{:S(2)}) async-start(bf16[16,2,8192]{2,1,0:T(2,128)(2,1)} %all_to_all.19), calls=%async_computation.2 | async-start | bytes 1048576 | tf_op jit(solution)/shard_map/all_to_all | solution.py:12
  140.8 3.4 %pad_maximum_fusion.1 = bf16[1,2,192,4096]{3,2,1,0:T(8,128)(2,1)} fusion(bf16[1,1,192,4096]{3,2,1,0:T(8,128)(2,1)} %fusion.1, bf16[1,1,192,4096]{3,2,1,0:T(8,128)(2,1)S(1)} %fusion), kind=kLoop, calls=%fused_computation.12 | loop fusion | flops 1572864 | bytes 6291456 | tf_op jit(solution)/shard_map/stack | solution.py:81
  144.1 7.6 %all-to-all-done.1 = bf16[16,2,8192]{2,1,0:T(2,128)(2,1)} async-done(((bf16[16,2,8192]{2,1,0:T(2,128)(2,1)}), bf16[16,2,8192]{2,1,0:T(2,128)(2,1)}, u32[]{:S(2)}, u32[]{:S(2)}) %all-to-all-start.1) | async-done | bytes 524320 | tf_op jit(solution)/shard_map/all_to_all | solution.py:12
  151.7 1.2 all_to_all.21
  153.0 1.1 convolution_convert_fusion.3
  154.1 1.1 convolution_convert_fusion.4
  (4 shorter events, 0.1 us)
Async XLA Ops:
  7.2 60.8 %copy-start = (bf16[1,192,4096]{2,1,0:T(8,128)(2,1)S(1)}, bf16[1,192,4096]{2,1,0:T(8,128)(2,1)}, u32[]{:S(2)}) copy-start(bf16[1,192,4096]{2,1,0:T(8,128)(2,1)} %param.11) | copy-start | bytes 4718596
  7.2 57.7 %all-gather.2.cloned.1.call-start = ((), (), s32[]{:S(2)}) async-start(), calls=%async_computation.3 | async-start | bytes 4718592 | tf_op jit(solution)/shard_map/all_gather | solution.py:28
  34.7 94.9 %reduce-scatter.2.cloned.1.call-start = ((), (), s32[]{:S(2)}) async-start(), calls=%async_computation.4 | async-start | bytes 9437184 | tf_op jit(solution)/shard_map/reduce_scatter | solution.py:38
  64.9 3.3 %copy-start.1 = (bf16[256,8192]{1,0:T(8,128)(2,1)S(1)}, bf16[256,8192]{1,0:T(8,128)(2,1)}, u32[]{:S(2)}) copy-start(bf16[256,8192]{1,0:T(8,128)(2,1)} %all-gather.2.cloned.1.call-done) | copy-start | bytes 12582916
  68.2 1.9 %copy-start.3 = (bf16[1,2,192,4096]{3,2,1,0:T(8,128)(2,1)S(1)}, bf16[1,2,192,4096]{3,2,1,0:T(8,128)(2,1)}, u32[]{:S(2)}) copy-start(bf16[1,2,192,4096]{3,2,1,0:T(8,128)(2,1)} %param.10) | copy-start | bytes 9437188
  77.0 5.7 %copy-start.2 = (bf16[256,8192]{1,0:T(8,128)(2,1)S(1)}, bf16[256,8192]{1,0:T(8,128)(2,1)}, u32[]{:S(2)}) copy-start(bf16[256,8192]{1,0:T(8,128)(2,1)} %all-gather.2.cloned.1.call-done) | copy-start | bytes 12582916
  133.8 18.0 %all-to-all-start.1 = ((bf16[16,2,8192]{2,1,0:T(2,128)(2,1)}), bf16[16,2,8192]{2,1,0:T(2,128)(2,1)}, u32[]{:S(2)}, u32[]{:S(2)}) async-start(bf16[16,2,8192]{2,1,0:T(2,128)(2,1)} %all_to_all.19), calls=%async_computation.2 | async-start | bytes 1048576 | tf_op jit(solution)/shard_map/all_to_all | solution.py:12
Sparse Core Ops, SparseCore 0:
  34.8 30.0 all-gather.1
  77.1 52.3 reduce-scatter.1
where the time goes:
time: 163 us; the launch traced here: 162 us
  waiting for transfers between devices  82.9 us (51%)
  blocking collectives  19.3 us (12%)
  matrix products  19.1 us (12%)
  between operations  14.2 us (9%)
  other arithmetic  12 us (7%)
  local copies, waits for them, and re-layouts  7.46 us (5%)
  starting transfers between devices  7.08 us (4%)
    reduce_scatter x1, waiting for transfers between devices, in_one_piece_3(): lax.psum_scatter(both, axis, scatter_dimension=dim, tiled=True)  45.1 us
    all_gather x1, waiting for transfers between devices, in_one_piece_2(): lax.all_gather(both, axis, axis=dim, tiled=True)  30.2 us
    all_to_all x1, blocking collectives, in_one_piece(): lax.all_to_all(both, axis, split_axis=split_dim, concat_axis=concat_dim,...  19.3 us
    all_to_all x1, waiting for transfers between devices, in_one_piece(): lax.all_to_all(both, axis, split_axis=split_dim, concat_axis=concat_dim,...  7.63 us
    all_to_all x1, starting transfers between devices, in_one_piece(): lax.all_to_all(both, axis, split_axis=split_dim, concat_axis=concat_dim,...  7 us
    all_to_all x4, local copies, waits for them, and re-layouts, in_one_piece(): lax.all_to_all(both, axis, split_axis=split_dim, concat_axis=concat_dim,...  4.74 us
    concatenate x1, other arithmetic, in_one_piece_3(): both = jnp.concatenate(arrays, axis=along)  3.8 us
    dot_general x1, matrix products, expert_slice(): jnp.einsum('rf,rd->fd', up_grad, routed, preferred_element_type=jnp.float32)  3.37 us
  transfers between devices with their start and end apart: 3, of which 3 were waited for; matrix products, arithmetic and copies ran while one was open for 7% of the time, Pallas kernels for 0%

commit v1 on v0

v1 whole, which is shorter than its diff:
```python
import functools

import jax
import jax.numpy as jnp
from jax import lax
from jax.experimental import pallas as pl
from jax.experimental.pallas import tpu as pltpu
from jax.sharding import PartitionSpec as P

CAP = 2
PIECES = 8
BF16 = jnp.bfloat16
F32 = jnp.float32
MESH = pl.DeviceIdType.MESH


def dot(a, b):
    return jnp.dot(a, b, preferred_element_type=F32)


def dot_nt(a, b):
    return lax.dot_general(a, b, (((1,), (1,)), ((), ())), preferred_element_type=F32)


def dot_tn(a, b):
    return lax.dot_general(a, b, (((0,), (0,)), ((), ())), preferred_element_type=F32)


def iota(shape, dim):
    return lax.broadcasted_iota(jnp.int32, shape, dim)


def kernel(
    experts,
    ids_ref,
    gates_ref,
    tok_hbm,
    cot_hbm,
    win_hbm,
    wdn_hbm,
    moe_hbm,
    tgr_hbm,
    gin_hbm,
    gdn_hbm,
    src,
    win,
    wdn,
    slab,
    land,
    x,
    act,
    hid,
    part,
    mate,
    summed,
    far,
    near,
    gin,
    gdn,
    outs,
    in_sem,
    out_sem,
    own_sem,
    a2a_send,
    a2a_recv,
    ag_send,
    ag_recv,
    rs_send,
    rs_recv,
):
    rows, dim = tok_hbm.shape
    width = dim // PIECES
    ff = wdn_hbm.shape[1]
    group = CAP * PIECES
    slots = CAP * experts
    msg_rows = experts * group
    all_rows = 8 * slots

    t = lax.axis_index("tok")
    e = lax.axis_index("exp")
    up = lax.rem(t + 2, 8)
    opp = lax.rem(t + 4, 8)
    dn = lax.rem(t + 6, 8)
    mate_t = t + 1 - 2 * lax.rem(t, 2)

    barrier = pltpu.get_barrier_semaphore()
    for k in range(1, experts):
        pl.semaphore_signal(
            barrier, inc=1, device_id=(t, lax.rem(e + k, experts)), device_id_type=MESH
        )
    for other in (up, dn, mate_t):
        pl.semaphore_signal(barrier, inc=1, device_id=(other, e), device_id_type=MESH)

    loads = []
    for q, hbm in enumerate((tok_hbm, cot_hbm)):
        group_loads = []
        for j in range(PIECES):
            copy = pltpu.make_async_copy(
                hbm.at[:, pl.ds(j * width, width)],
                src.at[q, pl.ds(j * rows, rows)],
                in_sem.at[q * PIECES + j],
            )
            copy.start()
            group_loads.append(copy)
        loads.append(group_loads)
    load_win = pltpu.make_async_copy(win_hbm.at[0], win, in_sem.at[2 * PIECES])
    load_wdn = pltpu.make_async_copy(wdn_hbm.at[0], wdn, in_sem.at[2 * PIECES + 1])
    load_win.start()
    load_wdn.start()

    def remote(a, b, ssem, rsem, dev_t, dev_e):
        return pltpu.make_async_remote_copy(
            src_ref=a,
            dst_ref=b,
            send_sem=ssem,
            recv_sem=rsem,
            device_id=(dev_t, dev_e),
            device_id_type=MESH,
        )

    ids = ids_ref[...]
    gates = gates_ref[...].astype(F32)
    row_e = iota((msg_rows, rows), 0) // group
    hits = jnp.zeros((msg_rows, rows), F32)
    weights = jnp.zeros((msg_rows, rows), F32)
    for k in range(ids.shape[0]):
        same = ids[k : k + 1, :] == row_e
        hits = hits + jnp.where(same, 1.0, 0.0)
        weights = weights + jnp.where(same, gates[k : k + 1, :], 0.0)
    earlier = jnp.where(iota((rows, rows), 0) < iota((rows, rows), 1), 1.0, 0.0)
    before = dot(hits.astype(BF16), earlier.astype(BF16))
    slot_of_row = lax.rem(iota((msg_rows, rows), 0), CAP).astype(F32)
    here = before == slot_of_row
    spread = jnp.where(
        iota((rows, PIECES * rows), 0) == lax.rem(iota((rows, PIECES * rows), 1), rows), 1.0, 0.0
    ).astype(BF16)
    wide = (msg_rows, PIECES * rows)
    same_piece = lax.rem(iota(wide, 0), group) // CAP == iota(wide, 1) // rows

    def table(values):
        full = dot(jnp.where(here, values, 0.0).astype(BF16), spread)
        return jnp.where(same_piece, full, 0.0).astype(BF16)

    pick_table = table(hits)
    for copy in loads[0]:
        copy.wait()
    slab[0] = (
        dot(pick_table, src[0]).astype(BF16).reshape(experts, group, width)
    )
    pl.semaphore_wait(barrier, experts + 2)

    def exchange(n):
        copies = []
        for k in range(1, experts):
            peer = lax.rem(e + k, experts)
            copies.append(
                remote(
                    slab.at[n, peer], land.at[n, e], a2a_send.at[n], a2a_recv.at[n], t, peer
                )
            )
        for copy in copies:
            copy.start()
        pltpu.make_async_copy(slab.at[n, e], land.at[n, e], own_sem.at[n]).start()

    def exchanged(n):
        pltpu.make_async_copy(slab.at[n, e], land.at[n, e], own_sem.at[n]).wait()
        some = pl.ds(0, experts - 1)
        whole = remote(
            slab.at[n, some], land.at[n, some], a2a_send.at[n], a2a_recv.at[n], t, e
        )
        whole.wait_send()
        whole.wait_recv()

    exchange(0)
    weight_table = table(weights)
    for copy in loads[1]:
        copy.wait()
    slab[1] = dot(weight_table, src[1]).astype(BF16).reshape(experts, group, width)
    exchange(1)

    square = (msg_rows, msg_rows)
    r0, r1 = iota(square, 0), iota(square, 1)
    gathers = jnp.where(
        r1 == lax.rem(r0, slots) // CAP * group + r0 // slots * CAP + lax.rem(r0, CAP), 1.0, 0.0
    ).astype(BF16)
    scatters = jnp.where(
        r1 == lax.rem(r0, group) // CAP * slots + r0 // group * CAP + lax.rem(r0, CAP), 1.0, 0.0
    ).astype(BF16)

    def take_rows(q):
        exchanged(q)
        own = dot(gathers, land[q].reshape(msg_rows, width)).astype(BF16)
        own = own.reshape(PIECES, 2, experts, width)
        for j in range(PIECES):
            x[q, t, :, :, j * width : (j + 1) * width] = own[j]

    def ag(q, n):
        block, half, dev = (
            (t, 0, up),
            (t, 1, up),
            (dn, 0, up),
            (t, 1, dn),
            (t, 0, dn),
            (up, 1, dn),
            (t, None, mate_t),
            (dn, 0, mate_t),
            (up, 1, mate_t),
            (dn, 1, mate_t),
            (up, 0, mate_t),
            (opp, 0, mate_t),
            (opp, 1, mate_t),
        )[n]
        ref = x.at[q, block] if half is None else x.at[q, block, half]
        return remote(ref, ref, ag_send.at[q, n], ag_recv.at[q, n], dev, e)

    def ag_arrived(q, n):
        mate_blocks = [lax.rem(mate_t + d, 8) for d in (0, 6, 2, 6, 2, 4, 4)]
        block, half = (
            (dn, 0),
            (dn, 1),
            (opp, 0),
            (up, 1),
            (up, 0),
            (opp, 1),
            (mate_blocks[0], None),
            (mate_blocks[1], 0),
            (mate_blocks[2], 1),
            (mate_blocks[3], 1),
            (mate_blocks[4], 0),
            (mate_blocks[5], 0),
            (mate_blocks[6], 1),
        )[n]
        ref = x.at[q, block] if half is None else x.at[q, block, half]
        remote(ref, ref, ag_send.at[q, n], ag_recv.at[q, n], t, e).wait_recv()

    def ag_first(q):
        for n in (0, 3, 1, 4, 6):
            ag(q, n).start()

    def ag_relay(q):
        ag_arrived(q, 0)
        ag(q, 2).start()
        ag(q, 7).start()
        ag_arrived(q, 3)
        ag(q, 5).start()
        ag(q, 8).start()

    def ag_second(q):
        ag_arrived(q, 1)
        ag(q, 9).start()
        ag_arrived(q, 4)
        ag(q, 10).start()

    def ag_last(q):
        ag_arrived(q, 2)
        ag(q, 11).start()
        ag_arrived(q, 5)
        ag(q, 12).start()
        for n in range(6, 13):
            ag_arrived(q, n)

    def rs(q, n):
        if n >= 6:
            d = (2, 1, 3, 0)[n - 6]
            a, b, dev = part.at[q, lax.rem(mate_t + 2 * d, 8)], mate.at[q, d], mate_t
        else:
            a, b, dev = (
                (summed.at[q, 2, 0], far.at[q, 0], up),
                (summed.at[q, 1, 1], near.at[q, 0, 1], up),
                (summed.at[q, 1, 0], near.at[q, 0, 0], up),
                (summed.at[q, 2, 1], far.at[q, 1], dn),
                (summed.at[q, 3, 0], near.at[q, 1, 0], dn),
                (summed.at[q, 3, 1], near.at[q, 1, 1], dn),
            )[n]
        return remote(a, b, rs_send.at[q, n], rs_recv.at[q, n], dev, e)

    def chip_sum(q, n):
        rs(q, n).wait_recv()
        d = (2, 1, 3, 0)[n - 6]
        own = part[q, lax.rem(t + 2 * d, 8)].astype(F32)
        summed[q, d] = (own + mate[q, d].astype(F32)).astype(BF16)

    def rs_pair(q):
        for n in range(6, 10):
            rs(q, n).start()

    def rs_first(q):
        chip_sum(q, 6)
        rs(q, 0).start()
        rs(q, 3).start()
        chip_sum(q, 7)
        rs(q, 1).start()
        chip_sum(q, 8)
        rs(q, 4).start()

    def rs_second(q):
        for way, d, half, n in ((0, 1, 0, 0), (1, 3, 1, 3)):
            rs(q, n).wait_recv()
            total = summed[q, d, half].astype(F32) + far[q, way].astype(F32)
            summed[q, d, half] = total.astype(BF16)
            rs(q, n + 2).start()

    def rs_last(q):
        rs(q, 9).wait_recv()
        for n in (1, 2, 4, 5):
            rs(q, n).wait_recv()
        total = part[q, t].astype(F32) + mate[q, 0].astype(F32)
        total = total + near[q, 0].astype(F32) + near[q, 1].astype(F32)
        total = total.astype(BF16)
        stacked = jnp.concatenate(
            [
                total[:, :, j * width : (j + 1) * width].reshape(slots, width)
                for j in range(PIECES)
            ],
            axis=0,
        )
        slab[2 + q] = dot(scatters, stacked).astype(BF16).reshape(experts, group, width)
        exchange(2 + q)

    def combine(q, placed):
        exchanged(2 + q)
        rows_out = dot_tn(placed, land[2 + q].reshape(msg_rows, width)).astype(BF16)
        for j in range(PIECES):
            outs[q, :, j * width : (j + 1) * width] = rows_out[j * rows : (j + 1) * rows]
        copy = pltpu.make_async_copy(
            outs.at[q], (moe_hbm, tgr_hbm)[q], out_sem.at[q]
        )
        copy.start()
        return copy

    def columns(k):
        return pl.ds(pl.multiple_of(k * width, width), width)

    def over_columns(step):
        def body(k, carry):
            step(columns(k))
            return carry

        lax.fori_loop(0, PIECES, body, 0)

    take_rows(0)
    ag_first(0)
    take_rows(1)
    ag_relay(0)
    ag_first(1)
    ag_second(0)
    load_win.wait()
    load_wdn.wait()
    ag_last(0)

    act[...] = jnp.zeros_like(act)

    def forward(cols):
        piece = x[0, :, :, :, cols].reshape(all_rows, width)
        act[0] += dot_nt(win[0, :, cols], piece)
        act[1] += dot_nt(win[1, :, cols], piece)

    over_columns(forward)
    ag_relay(1)
    gate = act[0]
    hid[0] = (gate * jax.nn.sigmoid(gate) * act[1]).astype(BF16)

    def terms_out(cols):
        piece = dot_tn(hid[0], wdn[:, cols]).astype(BF16)
        part[0, :, :, :, cols] = piece.reshape(8, 2, experts, width)

    over_columns(terms_out)
    rs_pair(0)
    ag_second(1)
    rs_first(0)
    ag_last(1)

    def backward(cols):
        piece = x[1, :, :, :, cols].reshape(all_rows, width)
        act[2] += dot_nt(wdn[:, cols], piece)

    over_columns(backward)
    gate = act[0]
    sigmoid = jax.nn.sigmoid(gate)
    grad = act[2]
    hid[1] = (grad * act[1] * sigmoid * (1.0 + gate * (1.0 - sigmoid))).astype(BF16)
    hid[2] = (grad * (gate * sigmoid)).astype(BF16)
    rs_second(0)

    def terms_grad(cols):
        piece = dot_tn(hid[1], win[0, :, cols]) + dot_tn(hid[2], win[1, :, cols])
        part[1, :, :, :, cols] = piece.astype(BF16).reshape(8, 2, experts, width)

    over_columns(terms_grad)
    rs_pair(1)
    rs_first(1)
    rs_last(0)

    def weights_down(cols):
        piece = x[1, :, :, :, cols].reshape(all_rows, width)
        gdn[:, cols] = dot(hid[0], piece).astype(BF16)

    def weights_in(cols):
        piece = x[0, :, :, :, cols].reshape(all_rows, width)
        gin[0, :, cols] = dot(hid[1], piece).astype(BF16)
        gin[1, :, cols] = dot(hid[2], piece).astype(BF16)

    over_columns(weights_down)
    store_gdn = pltpu.make_async_copy(gdn, gdn_hbm.at[0], out_sem.at[2])
    store_gdn.start()
    rs_second(1)
    over_columns(weights_in)
    store_gin = pltpu.make_async_copy(gin, gin_hbm.at[0], out_sem.at[3])
    store_gin.start()
    store_moe = combine(0, weight_table)
    rs_last(1)
    store_tgr = combine(1, pick_table)

    for q in range(2):
        for n in range(13):
            ag(q, n).wait_send()
        for n in range(10):
            rs(q, n).wait_send()
    for copy in (store_gdn, store_gin, store_moe, store_tgr):
        copy.wait()


def body(tokens, cotangent, expert_ids, gate_weights, w_in, w_down):
    experts = lax.axis_size("exp")
    rows, dim = tokens.shape
    ff = w_down.shape[1]
    width = dim // PIECES
    group = CAP * PIECES
    any_space = pl.BlockSpec(memory_space=pl.ANY)
    vmem = pl.BlockSpec(memory_space=pltpu.VMEM)
    shape = jax.ShapeDtypeStruct
    dma = pltpu.SemaphoreType.DMA
    return pl.pallas_call(
        functools.partial(kernel, experts),
        out_shape=(
            shape(tokens.shape, BF16),
            shape(tokens.shape, BF16),
            shape(w_in.shape, BF16),
            shape(w_down.shape, BF16),
        ),
        in_specs=[vmem, vmem, any_space, any_space, any_space, any_space],
        out_specs=(any_space,) * 4,
        scratch_shapes=[
            pltpu.VMEM((2, PIECES * rows, width), BF16),
            pltpu.VMEM((2, ff, dim), BF16),
            pltpu.VMEM((ff, dim), BF16),
            pltpu.VMEM((4, experts, group, width), BF16),
            pltpu.VMEM((4, experts, group, width), BF16),
            pltpu.VMEM((2, 8, 2, experts, dim), BF16),
            pltpu.VMEM((3, ff, 16 * experts), F32),
            pltpu.VMEM((3, ff, 16 * experts), BF16),
            pltpu.VMEM((2, 8, 2, experts, dim), BF16),
            pltpu.VMEM((2, 4, 2, experts, dim), BF16),
            pltpu.VMEM((2, 4, 2, experts, dim), BF16),
            pltpu.VMEM((2, 2, experts, dim), BF16),
            pltpu.VMEM((2, 2, 2, experts, dim), BF16),
            pltpu.VMEM((2, ff, dim), BF16),
            pltpu.VMEM((ff, dim), BF16),
            pltpu.VMEM((2, rows, dim), BF16),
            dma((2 * PIECES + 2,)),
            dma((4,)),
            dma((4,)),
            dma((4,)),
            dma((4,)),
            dma((2, 13)),
            dma((2, 13)),
            dma((2, 10)),
            dma((2, 10)),
        ],
        compiler_params=pltpu.CompilerParams(
            collective_id=0, has_side_effects=True, vmem_limit_bytes=60 * 1024 * 1024
        ),
    )(expert_ids.T, gate_weights.T, tokens, cotangent, w_in, w_down)


def solution(mesh):
    placed = (
        P(("tok", "exp"), None),
        P(("tok", "exp"), None),
        P(("tok", "exp"), None),
        P(("tok", "exp"), None),
        P("exp", None, "tok", None),
        P("exp", "tok", None),
    )
    return jax.shard_map(
        body,
        mesh=mesh,
        in_specs=placed,
        out_specs=(
            P(("tok", "exp"), None),
            P(("tok", "exp"), None),
            P("exp", None, "tok", None),
            P("exp", "tok", None),
        ),
        check_vma=False,
    )
```

time: 163 us -> 74 us (0.45)
  waiting for transfers between devices: 82.9 us -> 0 us
  Pallas kernels: 0 us -> 63.3 us
  blocking collectives: 19.3 us -> 0 us
  matrix products: 19.1 us -> 0 us
  between operations: 14.2 us -> 0.64 us
  other arithmetic: 12 us -> 0 us
  starting transfers between devices: 7.08 us -> 0 us
    pallas_call x0 -> x1, Pallas kernels: none -> 63.3 us  [body(): pl.pallas_call(functools.partial(kernel, experts), out_shape=(shape(token...]
    reduce_scatter x1 -> x0, waiting for transfers between devices: 45.1 us -> none  [in_one_piece_3(): lax.psum_scatter(both, axis, scatter_dimension=dim, tiled=True)]
    all_gather x1 -> x0, waiting for transfers between devices: 30.2 us -> none  [in_one_piece_2(): lax.all_gather(both, axis, axis=dim, tiled=True)]
    all_to_all x1 -> x0, blocking collectives: 19.3 us -> none  [in_one_piece(): lax.all_to_all(both, axis, split_axis=split_dim, concat_axis=concat_dim,...]
    dot_general x13 -> x0, matrix products: 19.1 us -> none  [the longest x1 3.37 us: expert_slice(): jnp.einsum('rf,rd->fd', up_grad, routed, preferred_element_type=jnp.float32)]
    all_to_all x1 -> x0, waiting for transfers between devices: 7.63 us -> none  [in_one_piece(): lax.all_to_all(both, axis, split_axis=split_dim, concat_axis=concat_dim,...]
    all_to_all x1 -> x0, starting transfers between devices: 7 us -> none  [in_one_piece(): lax.all_to_all(both, axis, split_axis=split_dim, concat_axis=concat_dim,...]
    unnamed x9 -> x6, local copies, waits for them, and re-layouts: 2.17 us -> 8.91 us
  transfers between devices with their start and end apart: 3 -> 0, of which waited for: 3 -> 0; matrix products, arithmetic and copies ran while one was open for 7% -> 0% of each run, Pallas kernels for 0% -> 0%
where the time goes in v1:
time: 74 us; the launch traced here: 72.9 us
  Pallas kernels  63.3 us (86%)
  local copies, waits for them, and re-layouts  8.91 us (12%)
    pallas_call x1, Pallas kernels, body(): pl.pallas_call(functools.partial(kernel, experts), out_shape=(shape(token...  63.3 us
    unnamed x6, local copies, waits for them, and re-layouts  8.91 us

profile of v1, /device:TPU:0, one launch (start us, length us, event | category | flops | bytes accessed | tf_op | source)
XLA Modules:
  0.0 72.9 jit_solution(12651204784601819925)
XLA Ops:
  0.6 63.3 %shard_map.93 = (bf16[64,4096]{1,0:T(8,128)(2,1)}, bf16[64,4096]{1,0:T(8,128)(2,1)}, bf16[1,2,192,4096]{3,2,1,0:T(8,128)(2,1)}, bf16[1,192,4096]{2,1,0:T(8,128)(2,1)}) custom-call(s32[8,64]{1,0:T(8,128)} %bitcast.2, bf16[8,64]{1,0:T(8,128)(2,1)} %bitcast.3, bf16[64,4096]{1,0:T(8,128)(2,1)} %tok_hbm.1, bf16[64,4096]{1,0:T(8,128)(2,1)} %cot_hbm.1, ...), custom_call_target="tpu_custom_call" | custom-call | tf_op jit(solution)/shard_map/pallas_call | solution.py:433
  63.9 1.9 %copy.14 = bf16[64,4096]{1,0:T(8,128)(2,1)} copy(bf16[64,4096]{1,0:T(8,128)(2,1)} %get-tuple-element.8) | data formatting | bytes 1048576
  65.8 1.9 %copy.15 = bf16[64,4096]{1,0:T(8,128)(2,1)} copy(bf16[64,4096]{1,0:T(8,128)(2,1)} %get-tuple-element.9) | data formatting | bytes 1048576
  67.7 0.0 copy-start
  67.7 4.0 %copy.16 = bf16[1,2,192,4096]{3,2,1,0:T(8,128)(2,1)} copy(bf16[1,2,192,4096]{3,2,1,0:T(8,128)(2,1)} %get-tuple-element.10) | data formatting | bytes 6291456
  71.7 0.0 copy-done
  71.7 1.1 %copy.17 = bf16[1,192,4096]{2,1,0:T(8,128)(2,1)} copy(bf16[1,192,4096]{2,1,0:T(8,128)(2,1)S(1)} %copy-done) | data formatting | bytes 3145728
Async XLA Ops:
  67.7 4.0 %copy-start = (bf16[1,192,4096]{2,1,0:T(8,128)(2,1)S(1)}, bf16[1,192,4096]{2,1,0:T(8,128)(2,1)}, u32[]{:S(2)}) copy-start(bf16[1,192,4096]{2,1,0:T(8,128)(2,1)} %get-tuple-element.11) | copy-start | bytes 4718596

commit v2 on v0

v2 whole, which is shorter than its diff:
```python
import functools

import jax
import jax.numpy as jnp
from jax import lax
from jax.experimental import pallas as pl
from jax.experimental.pallas import tpu as pltpu
from jax.sharding import PartitionSpec as P

CAP = 2
PIECES = 8
BF16 = jnp.bfloat16
F32 = jnp.float32
VMEM_LIMIT = 61_270_000
SPLITS = (4, 2, 2, 4)
MESH = pl.DeviceIdType.MESH


def dot(a, b):
    return jnp.dot(a, b, preferred_element_type=F32)


def dot_nt(a, b):
    return lax.dot_general(a, b, (((1,), (1,)), ((), ())), preferred_element_type=F32)


def dot_tn(a, b):
    return lax.dot_general(a, b, (((0,), (0,)), ((), ())), preferred_element_type=F32)


def iota(shape, dim):
    return lax.broadcasted_iota(jnp.int32, shape, dim)


def kernel(
    experts,
    ids_hbm,
    gates_hbm,
    tok_hbm,
    cot_hbm,
    win_hbm,
    wdn_hbm,
    moe,
    tgr,
    gin,
    gdn,
    ids_ref,
    gates_ref,
    src,
    win,
    wdn,
    x,
    act,
    hid,
    hid_rows,
    part,
    mate,
    summed,
    far,
    near,
    back,
    in_sem,
    a2a_send,
    a2a_recv,
    ag_send,
    ag_recv,
    rs_send,
    rs_recv,
    *boxes,
):
    slab, land = boxes[:4], boxes[4:]
    rows, dim = tok_hbm.shape
    group = CAP * PIECES
    slots = CAP * experts
    msg_rows = experts * group
    all_rows = 8 * slots
    chunk = dim // 8

    t = lax.axis_index("tok")
    e = lax.axis_index("exp")
    up = lax.rem(t + 2, 8)
    opp = lax.rem(t + 4, 8)
    dn = lax.rem(t + 6, 8)
    mate_t = t + 1 - 2 * lax.rem(t, 2)

    side = 4 if experts == 16 else 1
    line = experts // side

    def steps(k):
        a, b = k // line, k % line
        return min(a, side - a) + min(b, line - b)

    peers = [
        lax.rem(e // line + k // line, side) * line + lax.rem(lax.rem(e, line) + k % line, line)
        for k in sorted(range(1, experts), key=steps, reverse=True)
    ]
    barrier = pltpu.get_barrier_semaphore()
    for peer in peers:
        pl.semaphore_signal(barrier, inc=1, device_id=(t, peer), device_id_type=MESH)
    for other in (up, dn, mate_t):
        pl.semaphore_signal(barrier, inc=1, device_id=(other, e), device_id_type=MESH)

    loads = [
        pltpu.make_async_copy(a, b, in_sem.at[i])
        for i, (a, b) in enumerate(
            (
                (ids_hbm, ids_ref),
                (gates_hbm, gates_ref),
                (tok_hbm, src.at[0]),
                (cot_hbm, src.at[1]),
                (win_hbm.at[0], win),
                (wdn_hbm.at[0], wdn),
            )
        )
    ]
    for copy in loads:
        copy.start()

    def remote(a, b, ssem, rsem, dev_t, dev_e):
        return pltpu.make_async_remote_copy(
            src_ref=a,
            dst_ref=b,
            send_sem=ssem,
            recv_sem=rsem,
            device_id=(dev_t, dev_e),
            device_id_type=MESH,
        )

    loads[0].wait()
    loads[1].wait()
    ids = ids_ref[...]
    gates = gates_ref[...].astype(F32)
    row_e = iota((msg_rows, rows), 0) // group
    hits = jnp.zeros((msg_rows, rows), F32)
    weights = jnp.zeros((msg_rows, rows), F32)
    for k in range(ids.shape[0]):
        same = ids[k : k + 1, :] == row_e
        hits = hits + jnp.where(same, 1.0, 0.0)
        weights = weights + jnp.where(same, gates[k : k + 1, :], 0.0)
    earlier = jnp.where(iota((rows, rows), 0) < iota((rows, rows), 1), 1.0, 0.0)
    before = dot(hits.astype(BF16), earlier.astype(BF16))
    slot_of_row = lax.rem(iota((msg_rows, rows), 0), CAP).astype(F32)
    here = before == slot_of_row
    picked = jnp.where(here, hits, 0.0).astype(BF16)
    weighted = jnp.where(here, weights, 0.0).astype(BF16)
    wide = (msg_rows, PIECES * rows)
    tall = wide[::-1]

    def ones_where(test):
        return jnp.where(test, 1.0, 0.0).astype(BF16)

    def table(values):
        spread = ones_where(
            iota((rows, wide[1]), 0) == lax.rem(iota((rows, wide[1]), 1), rows)
        )
        same = lax.rem(iota(wide, 0), group) // CAP == iota(wide, 1) // rows
        return jnp.where(same, dot(values, spread), 0.0).astype(BF16)

    def back_table(values):
        spread = ones_where(
            lax.rem(iota((wide[1], rows), 0), rows) == iota((wide[1], rows), 1)
        )
        same = lax.rem(iota(tall, 1), group) // CAP == iota(tall, 0) // rows
        return jnp.where(same, dot_nt(spread, values), 0.0).astype(BF16)

    def span(n, s):
        size = dim // SPLITS[n]
        return pl.ds(s * size, size), size // PIECES

    def fill(n, s, placed):
        start, width = span(n, s)[0].start, span(n, s)[1]
        pieces = jnp.concatenate(
            [src[n, :, start + j * width : start + (j + 1) * width] for j in range(PIECES)],
            axis=0,
        )
        slab[n][s] = dot(placed, pieces).astype(BF16).reshape(experts, group, width)

    def exchange(n, s):
        copies = [
            remote(
                slab[n].at[s, peer],
                land[n].at[s, e],
                a2a_send.at[n],
                a2a_recv.at[n, s],
                t,
                peer,
            )
            for peer in peers
        ]
        for copy in copies:
            copy.start()
        land[n][s, e] = slab[n][s, e]

    def exchanged(n, s):
        ref = land[n].at[s, pl.ds(0, experts - 1)]
        remote(ref, ref, a2a_send.at[n], a2a_recv.at[n, s], t, e).wait_recv()
        return land[n][s].reshape(msg_rows, span(n, s)[1])

    pick_table = table(picked)
    loads[2].wait()
    for s in range(SPLITS[0]):
        fill(0, s, pick_table)
    pl.semaphore_wait(barrier, experts + 2)
    for s in range(SPLITS[0]):
        exchange(0, s)
    weight_table = table(weighted)
    loads[3].wait()
    for s in range(SPLITS[1]):
        fill(1, s, weight_table)
    for s in range(SPLITS[1]):
        exchange(1, s)

    square = (msg_rows, msg_rows)
    r0, r1 = iota(square, 0), iota(square, 1)
    gathers = ones_where(
        r1 == lax.rem(r0, slots) // CAP * group + r0 // slots * CAP + lax.rem(r0, CAP)
    )
    scatters = ones_where(
        r1 == lax.rem(r0, group) // CAP * slots + r0 // group * CAP + lax.rem(r0, CAP)
    )

    def take_rows(q, s):
        start, width = span(q, s)[0].start, span(q, s)[1]
        own = dot(gathers, exchanged(q, s)).astype(BF16)
        own = own.reshape(PIECES, 2, experts, width)
        for j in range(PIECES):
            x[q, t, :, :, start + j * width : start + (j + 1) * width] = own[j]

    def ag_ref(q, s, block, half):
        cols = span(q, s)[0]
        if half is None:
            return x.at[q, block, :, :, cols]
        return x.at[q, block, half, :, cols]

    def ag(q, s, n):
        block, half, dev = (
            (t, 0, up),
            (t, 1, up),
            (dn, 0, up),
            (t, 1, dn),
            (t, 0, dn),
            (up, 1, dn),
            (t, None, mate_t),
            (dn, 0, mate_t),
            (up, 1, mate_t),
            (dn, 1, mate_t),
            (up, 0, mate_t),
            (opp, 0, mate_t),
            (opp, 1, mate_t),
        )[n]
        ref = ag_ref(q, s, block, half)
        return remote(ref, ref, ag_send.at[q], ag_recv.at[q, s, n % 3 if n < 6 else 3], dev, e)

    def ag_arrived(q, s, n):
        ref = x.at[q, pl.ds(0, 4 if n == 3 else 1), :, :, span(q, s)[0]]
        remote(ref, ref, ag_send.at[q], ag_recv.at[q, s, n], t, e).wait_recv()

    def ag_first(q, s):
        for n in (0, 3, 1, 4, 6):
            ag(q, s, n).start()

    def ag_relay(q, s):
        ag_arrived(q, s, 0)
        for n in (2, 5, 7, 8):
            ag(q, s, n).start()

    def ag_second(q, s):
        ag_arrived(q, s, 1)
        for n in (9, 10):
            ag(q, s, n).start()

    def ag_third(q, s):
        ag_arrived(q, s, 2)
        for n in (11, 12):
            ag(q, s, n).start()

    def ag_last(q, s):
        ag_arrived(q, s, 3)

    def rs(q, s, n):
        cols = span(2 + q, s)[0]
        if n >= 6:
            d = (2, 1, 3, 0)[n - 6]
            a = part.at[q, lax.rem(mate_t + 2 * d, 8), :, :, cols]
            b, dev = mate.at[q, d, :, :, cols], mate_t
        else:
            a, b, dev = (
                (summed.at[q, 2, 0, :, cols], far.at[q, 0, :, cols], up),
                (summed.at[q, 1, 1, :, cols], near.at[q, 0, 1, :, cols], up),
                (summed.at[q, 1, 0, :, cols], near.at[q, 0, 0, :, cols], up),
                (summed.at[q, 2, 1, :, cols], far.at[q, 1, :, cols], dn),
                (summed.at[q, 3, 0, :, cols], near.at[q, 1, 0, :, cols], dn),
                (summed.at[q, 3, 1, :, cols], near.at[q, 1, 1, :, cols], dn),
            )[n]
        kind = (0, 1, 1, 0, 1, 1, 2, 3, 3, 3)[n]
        return remote(a, b, rs_send.at[q], rs_recv.at[q, s, kind], dev, e)

    def rs_arrived(q, s, kind):
        ref = (far.at[q], near.at[q], mate.at[q, 0], mate.at[q, pl.ds(0, 3)])[kind]
        ref = ref.at[..., span(2 + q, s)[0]]
        remote(ref, ref, rs_send.at[q], rs_recv.at[q, s, kind], t, e).wait_recv()

    def rs_pair(q, s):
        for n in range(6, 10):
            rs(q, s, n).start()

    def chip_sum(q, s, d):
        cols = span(2 + q, s)[0]
        own = part[q, lax.rem(t + 2 * d, 8), :, :, cols].astype(F32)
        summed[q, d, :, :, cols] = (own + mate[q, d, :, :, cols].astype(F32)).astype(BF16)

    def rs_far(q, s):
        rs_arrived(q, s, 2)
        chip_sum(q, s, 2)
        rs(q, s, 0).start()
        rs(q, s, 3).start()

    def rs_near(q, s):
        rs_arrived(q, s, 3)
        chip_sum(q, s, 1)
        rs(q, s, 1).start()
        chip_sum(q, s, 3)
        rs(q, s, 4).start()

    def rs_second(q, s):
        cols = span(2 + q, s)[0]
        rs_arrived(q, s, 0)
        for way, d, half, n in ((0, 1, 0, 2), (1, 3, 1, 5)):
            total = summed[q, d, half, :, cols].astype(F32) + far[q, way, :, cols].astype(F32)
            summed[q, d, half, :, cols] = total.astype(BF16)
            rs(q, s, n).start()

    def rs_last(q, s):
        cols, width = span(2 + q, s)
        total = part[q, t, :, :, cols].astype(F32) + mate[q, 0, :, :, cols].astype(F32)
        rs_arrived(q, s, 1)
        total = total + near[q, 0, :, :, cols].astype(F32) + near[q, 1, :, :, cols].astype(F32)
        total = total.astype(BF16).reshape(slots, PIECES * width)
        stacked = jnp.concatenate(
            [total[:, j * width : (j + 1) * width] for j in range(PIECES)], axis=0
        )
        slab[2 + q][s] = dot(scatters, stacked).astype(BF16).reshape(experts, group, width)
        exchange(2 + q, s)

    def combine(q, s):
        start, width = span(2 + q, s)[0].start, span(2 + q, s)[1]
        rows_out = dot(back[1 - q], exchanged(2 + q, s)).astype(BF16)
        out = (moe, tgr)[q]
        for j in range(PIECES):
            out[:, start + j * width : start + (j + 1) * width] = rows_out[
                j * rows : (j + 1) * rows
            ]

    def over(first, count, step):
        def body(k, carry):
            step(pl.ds(pl.multiple_of(k * chunk, chunk), chunk))
            return carry

        if count == 1:
            step(pl.ds(first * chunk, chunk))
        else:
            lax.fori_loop(first, first + count, body, 0)

    def chunks(n, s, step):
        count = 8 // SPLITS[n]
        over(s * count, count, step)

    def forward(cols):
        piece = x[0, :, :, :, cols].reshape(all_rows, chunk)
        act[0] += dot_nt(win[0, :, cols], piece)
        act[1] += dot_nt(win[1, :, cols], piece)

    def terms_out(cols):
        piece = dot(hid_rows[0], wdn[:, cols]).astype(BF16)
        part[0, :, :, :, cols] = piece.reshape(8, 2, experts, chunk)

    def backward(cols):
        piece = x[1, :, :, :, cols].reshape(all_rows, chunk)
        act[2] += dot_nt(wdn[:, cols], piece)

    def terms_grad(cols):
        piece = dot(hid_rows[1], win[0, :, cols]) + dot(hid_rows[2], win[1, :, cols])
        part[1, :, :, :, cols] = piece.astype(BF16).reshape(8, 2, experts, chunk)

    def weights_down(cols):
        piece = x[1, :, :, :, cols].reshape(all_rows, chunk)
        gdn[0, :, cols] = dot(hid[0], piece).astype(BF16)

    def weights_in(cols):
        piece = x[0, :, :, :, cols].reshape(all_rows, chunk)
        gin[0, 0, :, cols] = dot(hid[1], piece).astype(BF16)
        gin[0, 1, :, cols] = dot(hid[2], piece).astype(BF16)

    def keep(i, value):
        hid[i] = value.astype(BF16)
        hid_rows[i] = value.T.astype(BF16)

    act[...] = jnp.zeros_like(act)
    for s in range(SPLITS[0]):
        take_rows(0, s)
        ag_first(0, s)
    ag_relay(0, 0)
    for s in range(SPLITS[1]):
        take_rows(1, s)
    for s in range(1, SPLITS[0]):
        ag_relay(0, s)
    for s in range(SPLITS[1]):
        ag_first(1, s)
    back[0] = back_table(picked)
    back[1] = back_table(weighted)
    loads[4].wait()
    loads[5].wait()
    for s in range(SPLITS[0]):
        ag_second(0, s)
    for s in range(SPLITS[0]):
        ag_third(0, s)
    for s in range(SPLITS[0]):
        ag_last(0, s)
        chunks(0, s, forward)
    ag_relay(1, 0)

    gate = act[0]
    keep(0, gate * jax.nn.sigmoid(gate) * act[1])
    for s in range(SPLITS[2]):
        chunks(2, s, terms_out)
        rs_pair(0, s)
    for s in range(1, SPLITS[1]):
        ag_relay(1, s)
    for s in range(SPLITS[1]):
        ag_second(1, s)
    for s in range(SPLITS[2]):
        rs_far(0, s)
        rs_near(0, s)
    for s in range(SPLITS[1]):
        ag_third(1, s)
        ag_last(1, s)
        chunks(1, s, backward)

    gate = act[0]
    sigmoid = jax.nn.sigmoid(gate)
    grad = act[2]
    keep(1, grad * act[1] * sigmoid * (1.0 + gate * (1.0 - sigmoid)))
    keep(2, grad * (gate * sigmoid))
    for s in range(SPLITS[2]):
        rs_second(0, s)
    last = SPLITS[3]
    for s in range(last):
        chunks(3, s, terms_grad)
        rs_pair(1, s)

    rs_far(1, 0)
    rs_near(1, 0)
    rs_far(1, 1)
    rs_near(1, 1)
    for s in range(2, last):
        rs_far(1, s)
        rs_second(1, s - 2)
    for s in range(SPLITS[2]):
        rs_last(0, s)
    for s in range(2, last):
        rs_near(1, s)
        if s < last - 1:
            rs_second(1, s)
    rs_last(1, 0)
    rs_second(1, last - 1)
    over(0, 8, weights_down)
    for s in range(1, last):
        rs_last(1, s)
    over(0, 8, weights_in)
    for s in range(SPLITS[2]):
        combine(0, s)
    for s in range(last - 1):
        combine(1, s)

    for q in range(2):
        ref = x.at[q, pl.ds(0, 7)]
        remote(ref, ref, ag_send.at[q], ag_recv.at[q, 0, 0], t, e).wait_send()
        remote(ref, ref, rs_send.at[q], rs_recv.at[q, 0, 0], t, e).wait_send()
    for n in range(4):
        ref = slab[n].at[:, pl.ds(0, experts - 1)]
        remote(ref, ref, a2a_send.at[n], a2a_recv.at[n, 0], t, e).wait_send()
    combine(1, last - 1)


def store(*refs):
    count = len(refs) // 2
    sem = refs[-1]
    copies = [
        pltpu.make_async_copy(a, b, sem.at[i])
        for i, (a, b) in enumerate(zip(refs[:count], refs[count : 2 * count]))
    ]
    for copy in copies:
        copy.start()
    for copy in copies:
        copy.wait()


def body(tokens, cotangent, expert_ids, gate_weights, w_in, w_down):
    experts = lax.axis_size("exp")
    rows, dim = tokens.shape
    ff = w_down.shape[1]
    group = CAP * PIECES
    hbm = pl.BlockSpec(memory_space=pltpu.HBM)
    vmem = pl.BlockSpec(memory_space=pltpu.VMEM)
    shape = jax.ShapeDtypeStruct
    dma = pltpu.SemaphoreType.DMA
    shapes = (tokens.shape, tokens.shape, w_in.shape, w_down.shape)
    most = max(SPLITS)
    boxes = [
        pltpu.VMEM((n, experts, group, dim // n // PIECES), BF16) for n in SPLITS
    ]
    results = pl.pallas_call(
        functools.partial(kernel, experts),
        out_shape=tuple(pltpu.VMEM(s, BF16) for s in shapes),
        in_specs=[hbm] * 6,
        out_specs=(vmem,) * 4,
        scratch_shapes=[
            pltpu.VMEM(expert_ids.shape[::-1], jnp.int32),
            pltpu.VMEM(expert_ids.shape[::-1], BF16),
            pltpu.VMEM((2, rows, dim), BF16),
            pltpu.VMEM((2, ff, dim), BF16),
            pltpu.VMEM((ff, dim), BF16),
            pltpu.VMEM((2, 8, 2, experts, dim), BF16),
            pltpu.VMEM((3, ff, 16 * experts), F32),
            pltpu.VMEM((3, ff, 16 * experts), BF16),
            pltpu.VMEM((3, 16 * experts, ff), BF16),
            pltpu.VMEM((2, 8, 2, experts, dim), BF16),
            pltpu.VMEM((2, 4, 2, experts, dim), BF16),
            pltpu.VMEM((2, 4, 2, experts, dim), BF16),
            pltpu.VMEM((2, 2, experts, dim), BF16),
            pltpu.VMEM((2, 2, 2, experts, dim), BF16),
            pltpu.VMEM((2, PIECES * rows, experts * group), BF16),
            dma((6,)),
            dma((4,)),
            dma((4, most)),
            dma((2,)),
            dma((2, max(SPLITS[:2]), 4)),
            dma((2,)),
            dma((2, max(SPLITS[2:]), 4)),
        ]
        + boxes * 2,
        compiler_params=pltpu.CompilerParams(
            collective_id=0, has_side_effects=True, vmem_limit_bytes=VMEM_LIMIT
        ),
    )(expert_ids.T, gate_weights.T, tokens, cotangent, w_in, w_down)
    return pl.pallas_call(
        store,
        out_shape=tuple(shape(s, BF16) for s in shapes),
        in_specs=[vmem] * 4,
        out_specs=(hbm,) * 4,
        scratch_shapes=[dma((4,))],
        compiler_params=pltpu.CompilerParams(vmem_limit_bytes=1024 * 1024),
    )(*results)


def solution(mesh):
    placed = (
        P(("tok", "exp"), None),
        P(("tok", "exp"), None),
        P(("tok", "exp"), None),
        P(("tok", "exp"), None),
        P("exp", None, "tok", None),
        P("exp", "tok", None),
    )
    return jax.shard_map(
        body,
        mesh=mesh,
        in_specs=placed,
        out_specs=(
            P(("tok", "exp"), None),
            P(("tok", "exp"), None),
            P("exp", None, "tok", None),
            P("exp", "tok", None),
        ),
        check_vma=False,
    )
```

time: 163 us -> 61.3 us (0.38)
  waiting for transfers between devices: 82.9 us -> 0 us
  Pallas kernels: 0 us -> 60.5 us
  blocking collectives: 19.3 us -> 0 us
  matrix products: 19.1 us -> 0 us
  between operations: 14.2 us -> 0.64 us
  other arithmetic: 12 us -> 0 us
  local copies, waits for them, and re-layouts: 7.46 us -> 0 us
  starting transfers between devices: 7.08 us -> 0 us
    pallas_call x0 -> x2, Pallas kernels: none -> 60.5 us  [the longest x1 58 us: body(): pl.pallas_call(functools.partial(kernel, experts), out_shape=tuple((pltpu...]
    reduce_scatter x1 -> x0, waiting for transfers between devices: 45.1 us -> none  [in_one_piece_3(): lax.psum_scatter(both, axis, scatter_dimension=dim, tiled=True)]
    all_gather x1 -> x0, waiting for transfers between devices: 30.2 us -> none  [in_one_piece_2(): lax.all_gather(both, axis, axis=dim, tiled=True)]
    all_to_all x1 -> x0, blocking collectives: 19.3 us -> none  [in_one_piece(): lax.all_to_all(both, axis, split_axis=split_dim, concat_axis=concat_dim,...]
    dot_general x13 -> x0, matrix products: 19.1 us -> none  [the longest x1 3.37 us: expert_slice(): jnp.einsum('rf,rd->fd', up_grad, routed, preferred_element_type=jnp.float32)]
    all_to_all x1 -> x0, waiting for transfers between devices: 7.63 us -> none  [in_one_piece(): lax.all_to_all(both, axis, split_axis=split_dim, concat_axis=concat_dim,...]
    all_to_all x1 -> x0, starting transfers between devices: 7 us -> none  [in_one_piece(): lax.all_to_all(both, axis, split_axis=split_dim, concat_axis=concat_dim,...]
    another operation x4 -> x0, other arithmetic: 6.62 us -> none  [the longest x1 3.36 us: expert_slice(): grad_in = jnp.stack([grad_gate, grad_up]).astype(jnp.bfloat16)]
  transfers between devices with their start and end apart: 3 -> 0, of which waited for: 3 -> 0; matrix products, arithmetic and copies ran while one was open for 7% -> 0% of each run, Pallas kernels for 0% -> 0%
where the time goes in v2:
time: 61.3 us; the launch traced here: 61.2 us
  Pallas kernels  60.5 us (99%)
  between operations  0.64 us (1%)
    pallas_call x1, Pallas kernels, body(): pl.pallas_call(functools.partial(kernel, experts), out_shape=tuple((pltpu...  58 us
    pallas_call x1, Pallas kernels, body(): pl.pallas_call(store, out_shape=tuple((shape(s, BF16) for s in shapes)),...  2.56 us

profile of v2, /device:TPU:0, one launch (start us, length us, event | category | flops | bytes accessed | tf_op | source)
XLA Modules:
  0.0 61.2 jit_solution(2039579531163779664)
XLA Ops:
  0.6 58.0 %shard_map.93 = (bf16[64,4096]{1,0:T(8,128)(2,1)S(1)}, bf16[64,4096]{1,0:T(8,128)(2,1)S(1)}, bf16[1,2,192,4096]{3,2,1,0:T(8,128)(2,1)S(1)}, bf16[1,192,4096]{2,1,0:T(8,128)(2,1)S(1)}) custom-call(s32[8,64]{1,0:T(8,128)} %bitcast.2, bf16[8,64]{1,0:T(8,128)(2,1)} %bitcast.3, bf16[64,4096]{1,0:T(8,128)(2,1)} %tok_hbm.1, bf16[64,4096]{1,0:T(8,128)(2,1)} %cot_hbm.1, ...), custom_call_target="tpu_custom_call" | custom-call | tf_op jit(solution)/shard_map/pallas_call | solution.py:512
  58.6 2.6 %shard_map.94 = (bf16[64,4096]{1,0:T(8,128)(2,1)}, bf16[64,4096]{1,0:T(8,128)(2,1)}, bf16[1,2,192,4096]{3,2,1,0:T(8,128)(2,1)}, bf16[1,192,4096]{2,1,0:T(8,128)(2,1)}) custom-call(bf16[64,4096]{1,0:T(8,128)(2,1)S(1)} %get-tuple-element.8.refs_0_, bf16[64,4096]{1,0:T(8,128)(2,1)S(1)} %get-tuple-element.9.refs_1_, ...), custom_call_target="tpu_custom_call" | custom-call | tf_op jit(solution)/shard_map/pallas_call | solution.py:546

commit v3 on v2

--- a/solution.py
+++ b/solution.py
@@ -12,7 +12,9 @@
 BF16 = jnp.bfloat16
 F32 = jnp.float32
 VMEM_LIMIT = 61_270_000
-SPLITS = (4, 2, 2, 4)
+AHEAD = 2
+BEHIND = 2
+SPLITS = (4, 4, 4, 4)
 MESH = pl.DeviceIdType.MESH
 
 
@@ -30,6 +32,10 @@
 
 def iota(shape, dim):
     return lax.broadcasted_iota(jnp.int32, shape, dim)
+
+
+def stream(n, s):
+    return sum(SPLITS[:n]) + s
 
 
 def kernel(
@@ -66,6 +72,22 @@
     ag_recv,
     rs_send,
     rs_recv,
+    ring,
+    ringland,
+    ring_send,
+    ring_recv,
+    spread_send,
+    spread_recv,
+    mate_send,
+    backslab,
+    backland,
+    backfar,
+    backnear,
+    back_send,
+    back_recv,
+    backring_send,
+    backring_recv,
+    backmate_send,
     *boxes,
 ):
     slab, land = boxes[:4], boxes[4:]
@@ -82,6 +104,7 @@
     opp = lax.rem(t + 4, 8)
     dn = lax.rem(t + 6, 8)
     mate_t = t + 1 - 2 * lax.rem(t, 2)
+    y = t // 2
 
     side = 4 if experts == 16 else 1
     line = experts // side
@@ -173,7 +196,11 @@
             [src[n, :, start + j * width : start + (j + 1) * width] for j in range(PIECES)],
             axis=0,
         )
-        slab[n][s] = dot(placed, pieces).astype(BF16).reshape(experts, group, width)
+        message = dot(placed, pieces).astype(BF16).reshape(experts, group, width)
+        if n == 0 and s < AHEAD:
+            ring[s, y] = message
+        else:
+            slab[n][s] = message
 
     def exchange(n, s):
         copies = [
@@ -181,7 +208,7 @@
                 slab[n].at[s, peer],
                 land[n].at[s, e],
                 a2a_send.at[n],
-                a2a_recv.at[n, s],
+                a2a_recv.at[stream(n, s)],
                 t,
                 peer,
             )
@@ -193,15 +220,78 @@
 
     def exchanged(n, s):
         ref = land[n].at[s, pl.ds(0, experts - 1)]
-        remote(ref, ref, a2a_send.at[n], a2a_recv.at[n, s], t, e).wait_recv()
+        remote(ref, ref, a2a_send.at[n], a2a_recv.at[stream(n, s)], t, e).wait_recv()
         return land[n][s].reshape(msg_rows, span(n, s)[1])
+
+    def ring_copy(s, n):
+        d, half, dev = (
+            (0, 0, up),
+            (0, 1, up),
+            (3, 0, up),
+            (0, 1, dn),
+            (0, 0, dn),
+            (1, 1, dn),
+        )[n]
+        count = experts // 2
+        ref = ring.at[s, lax.rem(y + d, 4), pl.ds(half * count, count)]
+        return remote(ref, ref, ring_send, ring_recv.at[s, n % 3], dev, e)
+
+    def ring_arrived(s, kind):
+        ref = ring.at[s, 0]
+        remote(ref, ref, ring_send, ring_recv.at[s, kind], t, e).wait_recv()
+
+    def ring_first():
+        for pair in ((0, 3), (1, 4)):
+            for s in range(AHEAD):
+                for n in pair:
+                    ring_copy(s, n).start()
+
+    def spread(s, d):
+        block = lax.rem(y + d, 4)
+        copies = [
+            remote(
+                ring.at[s, block, peer],
+                ringland.at[s, d, e],
+                spread_send,
+                spread_recv.at[s, d],
+                t,
+                peer,
+            )
+            for peer in peers
+        ]
+        for copy in copies:
+            copy.start()
+        ringland[s, d, e] = ring[s, block, e]
+
+    def ring_relay(s):
+        ring_arrived(s, 0)
+        for n in (2, 5):
+            ring_copy(s, n).start()
+
+    def ring_near(s):
+        ring_arrived(s, 1)
+        spread(s, 1)
+        spread(s, 3)
+
+    def ring_last(s):
+        ring_arrived(s, 2)
+        spread(s, 2)
+
+    def ring_take(s, d):
+        ref = ringland.at[s, d, pl.ds(0, experts - 1)]
+        remote(ref, ref, spread_send, spread_recv.at[s, d], t, e).wait_recv()
+        block = lax.rem(t + 2 * d, 8)
+        put_rows(0, s, block, ringland[s, d])
+        ref = x.at[0, block, :, :, span(0, s)[0]]
+        remote(ref, ref, mate_send, ag_recv.at[stream(0, s), 3], mate_t, e).start()
 
     pick_table = table(picked)
     loads[2].wait()
     for s in range(SPLITS[0]):
         fill(0, s, pick_table)
     pl.semaphore_wait(barrier, experts + 2)
-    for s in range(SPLITS[0]):
+    ring_first()
+    for s in range(AHEAD, SPLITS[0]):
         exchange(0, s)
     weight_table = table(weighted)
     loads[3].wait()
@@ -209,6 +299,8 @@
         fill(1, s, weight_table)
     for s in range(SPLITS[1]):
         exchange(1, s)
+    for s in range(AHEAD):
+        spread(s, 0)
 
     square = (msg_rows, msg_rows)
     r0, r1 = iota(square, 0), iota(square, 1)
@@ -219,12 +311,15 @@
         r1 == lax.rem(r0, group) // CAP * slots + r0 // group * CAP + lax.rem(r0, CAP)
     )
 
-    def take_rows(q, s):
+    def put_rows(q, s, block, message):
         start, width = span(q, s)[0].start, span(q, s)[1]
-        own = dot(gathers, exchanged(q, s)).astype(BF16)
+        own = dot(gathers, message.reshape(msg_rows, width)).astype(BF16)
         own = own.reshape(PIECES, 2, experts, width)
         for j in range(PIECES):
-            x[q, t, :, :, start + j * width : start + (j + 1) * width] = own[j]
+            x[q, block, :, :, start + j * width : start + (j + 1) * width] = own[j]
+
+    def take_rows(q, s):
+        put_rows(q, s, t, exchanged(q, s))
 
     def ag_ref(q, s, block, half):
         cols = span(q, s)[0]
@@ -249,11 +344,11 @@
             (opp, 1, mate_t),
         )[n]
         ref = ag_ref(q, s, block, half)
-        return remote(ref, ref, ag_send.at[q], ag_recv.at[q, s, n % 3 if n < 6 else 3], dev, e)
+        return remote(ref, ref, ag_send.at[q], ag_recv.at[stream(q, s), n % 3 if n < 6 else 3], dev, e)
 
     def ag_arrived(q, s, n):
         ref = x.at[q, pl.ds(0, 4 if n == 3 else 1), :, :, span(q, s)[0]]
-        remote(ref, ref, ag_send.at[q], ag_recv.at[q, s, n], t, e).wait_recv()
+        remote(ref, ref, ag_send.at[q], ag_recv.at[stream(q, s), n], t, e).wait_recv()
 
     def ag_first(q, s):
         for n in (0, 3, 1, 4, 6):
@@ -276,6 +371,9 @@
 
     def ag_last(q, s):
         ag_arrived(q, s, 3)
+
+    last = SPLITS[3]
+    behind = last - BEHIND
 
     def rs(q, s, n):
         cols = span(2 + q, s)[0]
@@ -293,12 +391,13 @@
                 (summed.at[q, 3, 1, :, cols], near.at[q, 1, 1, :, cols], dn),
             )[n]
         kind = (0, 1, 1, 0, 1, 1, 2, 3, 3, 3)[n]
-        return remote(a, b, rs_send.at[q], rs_recv.at[q, s, kind], dev, e)
+        sem = backmate_send if q == 1 and s >= behind else rs_send.at[q]
+        return remote(a, b, sem, rs_recv.at[stream(2 + q, s) - stream(2, 0), kind], dev, e)
 
     def rs_arrived(q, s, kind):
         ref = (far.at[q], near.at[q], mate.at[q, 0], mate.at[q, pl.ds(0, 3)])[kind]
         ref = ref.at[..., span(2 + q, s)[0]]
-        remote(ref, ref, rs_send.at[q], rs_recv.at[q, s, kind], t, e).wait_recv()
+        remote(ref, ref, rs_send.at[q], rs_recv.at[stream(2 + q, s) - stream(2, 0), kind], t, e).wait_recv()
 
     def rs_pair(q, s):
         for n in range(6, 10):
@@ -330,21 +429,99 @@
             summed[q, d, half, :, cols] = total.astype(BF16)
             rs(q, s, n).start()
 
+    def as_message(total, width):
+        total = total.astype(BF16).reshape(slots, PIECES * width)
+        stacked = jnp.concatenate(
+            [total[:, j * width : (j + 1) * width] for j in range(PIECES)], axis=0
+        )
+        return dot(scatters, stacked).astype(BF16).reshape(experts, group, width)
+
+    def back_spread(d):
+        for s in range(behind, last):
+            cols, width = span(3, s)
+            b = s - behind
+            if d != 3 and d != 0:
+                rs_arrived(1, s, 2 if d == 2 else 3)
+            own = part[1, lax.rem(t + 2 * d, 8), :, :, cols].astype(F32)
+            backslab[b, d] = as_message(own + mate[1, d, :, :, cols].astype(F32), width)
+            copies = [
+                remote(
+                    backslab.at[b, d, peer],
+                    backland.at[b, d, e],
+                    back_send,
+                    back_recv.at[b, d],
+                    t,
+                    peer,
+                )
+                for peer in peers
+            ]
+            for copy in copies:
+                copy.start()
+            backland[b, d, e] = backslab[b, d, e]
+
+    def back_arrived(s, d):
+        ref = backland.at[s - behind, d, pl.ds(0, experts - 1)]
+        remote(ref, ref, back_send, back_recv.at[s - behind, d], t, e).wait_recv()
+
+    low, high = pl.ds(0, experts // 2), pl.ds(experts // 2, experts // 2)
+
+    def back_ring(s, d, half, ref, kind, dev):
+        remote(
+            backland.at[s - behind, d, half],
+            ref,
+            backring_send,
+            backring_recv.at[s - behind, kind],
+            dev,
+            e,
+        ).start()
+
+    def back_ring_arrived(s, kind):
+        ref = backnear.at[s - behind] if kind else backland.at[s - behind, 0]
+        remote(ref, ref, backring_send, backring_recv.at[s - behind, kind], t, e).wait_recv()
+
+    def back_far(s):
+        b = s - behind
+        back_arrived(s, 2)
+        back_ring(s, 2, low, backfar.at[b, 0], 0, up)
+        back_ring(s, 2, high, backfar.at[b, 1], 0, dn)
+
+    def back_near(s):
+        b = s - behind
+        back_arrived(s, 1)
+        back_ring(s, 1, high, backnear.at[b, 0, high], 1, up)
+        back_arrived(s, 3)
+        back_ring(s, 3, low, backnear.at[b, 1, low], 1, dn)
+
+    def back_second(s):
+        b = s - behind
+        back_ring_arrived(s, 0)
+        for way, d, half, dev in ((0, 1, low, up), (1, 3, high, dn)):
+            total = backland[b, d, half].astype(F32) + backfar[b, way].astype(F32)
+            backland[b, d, half] = total.astype(BF16)
+            back_ring(s, d, half, backnear.at[b, way, half], 1, dev)
+
+    def back_last(s):
+        b = s - behind
+        back_arrived(s, 0)
+        own = backland[b, 0].astype(F32)
+        back_ring_arrived(s, 1)
+        total = own + backnear[b, 0].astype(F32) + backnear[b, 1].astype(F32)
+        put_out(1, s, total.astype(BF16).reshape(msg_rows, span(3, s)[1]))
+
     def rs_last(q, s):
         cols, width = span(2 + q, s)
         total = part[q, t, :, :, cols].astype(F32) + mate[q, 0, :, :, cols].astype(F32)
         rs_arrived(q, s, 1)
         total = total + near[q, 0, :, :, cols].astype(F32) + near[q, 1, :, :, cols].astype(F32)
-        total = total.astype(BF16).reshape(slots, PIECES * width)
-        stacked = jnp.concatenate(
-            [total[:, j * width : (j + 1) * width] for j in range(PIECES)], axis=0
-        )
-        slab[2 + q][s] = dot(scatters, stacked).astype(BF16).reshape(experts, group, width)
+        slab[2 + q][s] = as_message(total, width)
         exchange(2 + q, s)
 
     def combine(q, s):
+        put_out(q, s, exchanged(2 + q, s))
+
+    def put_out(q, s, message):
         start, width = span(2 + q, s)[0].start, span(2 + q, s)[1]
-        rows_out = dot(back[1 - q], exchanged(2 + q, s)).astype(BF16)
+        rows_out = dot(back[1 - q], message).astype(BF16)
         out = (moe, tgr)[q]
         for j in range(PIECES):
             out[:, start + j * width : start + (j + 1) * width] = rows_out[
@@ -396,43 +573,70 @@
         hid_rows[i] = value.T.astype(BF16)
 
     act[...] = jnp.zeros_like(act)
-    for s in range(SPLITS[0]):
+    for s in range(AHEAD):
+        ring_relay(s)
+    later = range(AHEAD, SPLITS[0])
+    for s in later:
         take_rows(0, s)
         ag_first(0, s)
-    ag_relay(0, 0)
+    for s in range(AHEAD):
+        ring_near(s)
     for s in range(SPLITS[1]):
         take_rows(1, s)
-    for s in range(1, SPLITS[0]):
+    for s in later:
         ag_relay(0, s)
+        if s == AHEAD:
+            for a in range(AHEAD):
+                ring_last(a)
     for s in range(SPLITS[1]):
         ag_first(1, s)
+    for s in range(AHEAD):
+        ring_take(s, 0)
+    for s in later:
+        ag_second(0, s)
     back[0] = back_table(picked)
     back[1] = back_table(weighted)
+    for s in later:
+        ag_third(0, s)
+    for s in range(AHEAD):
+        ring_take(s, 1)
+        ring_take(s, 3)
     loads[4].wait()
     loads[5].wait()
-    for s in range(SPLITS[0]):
-        ag_second(0, s)
-    for s in range(SPLITS[0]):
-        ag_third(0, s)
-    for s in range(SPLITS[0]):
+    for s in later:
         ag_last(0, s)
         chunks(0, s, forward)
     ag_relay(1, 0)
+    for s in range(AHEAD):
+        ring_take(s, 2)
+    ag_relay(1, 1)
+    for s in range(AHEAD):
+        ag_last(0, s)
+        chunks(0, s, forward)
+    ag_relay(1, 2)
 
     gate = act[0]
     keep(0, gate * jax.nn.sigmoid(gate) * act[1])
     for s in range(SPLITS[2]):
         chunks(2, s, terms_out)
         rs_pair(0, s)
-    for s in range(1, SPLITS[1]):
-        ag_relay(1, s)
+        if s == 1:
+            ag_relay(1, 3)
+        if s >= 2:
+            rs_far(0, s - 2)
     for s in range(SPLITS[1]):
         ag_second(1, s)
-    for s in range(SPLITS[2]):
-        rs_far(0, s)
-        rs_near(0, s)
+    rs_far(0, 2)
+    rs_far(0, 3)
+    rs_near(0, 0)
+    rs_near(0, 1)
+    ag_third(1, 0)
+    ag_third(1, 1)
+    rs_near(0, 2)
+    rs_near(0, 3)
     for s in range(SPLITS[1]):
-        ag_third(1, s)
+        if s < 2:
+            ag_third(1, s + 2)
         ag_last(1, s)
         chunks(1, s, backward)
 
@@ -441,53 +645,79 @@
     grad = act[2]
     keep(1, grad * act[1] * sigmoid * (1.0 + gate * (1.0 - sigmoid)))
     keep(2, grad * (gate * sigmoid))
-    for s in range(SPLITS[2]):
-        rs_second(0, s)
-    last = SPLITS[3]
     for s in range(last):
         chunks(3, s, terms_grad)
         rs_pair(1, s)
-
-    rs_far(1, 0)
-    rs_near(1, 0)
-    rs_far(1, 1)
-    rs_near(1, 1)
-    for s in range(2, last):
+        if s < 2:
+            rs_second(0, s)
+        if s >= 2 and s - 2 < behind:
+            rs_far(1, s - 2)
+    rs_second(0, 2)
+    for s in range(2, behind):
         rs_far(1, s)
-        rs_second(1, s - 2)
+    for s in range(min(2, behind)):
+        rs_near(1, s)
+    back_spread(2)
+    rs_second(0, 3)
+    back_spread(1)
+    back_spread(3)
+    over(0, 4, weights_down)
+    for s in range(min(2, behind)):
+        rs_second(1, s)
+    back_spread(0)
+    for s in range(2, behind):
+        rs_near(1, s)
+    over(4, 4, weights_down)
+    back_far(behind)
+    over(0, 4, weights_in)
+    for s in range(behind + 1, last):
+        back_far(s)
     for s in range(SPLITS[2]):
         rs_last(0, s)
-    for s in range(2, last):
-        rs_near(1, s)
-        if s < last - 1:
-            rs_second(1, s)
-    rs_last(1, 0)
-    rs_second(1, last - 1)
-    over(0, 8, weights_down)
-    for s in range(1, last):
+    for s in range(2, behind):
+        rs_second(1, s)
+    for s in range(behind, last):
+        back_near(s)
+    for s in range(behind):
         rs_last(1, s)
-    over(0, 8, weights_in)
+    back_second(behind)
+    over(4, 4, weights_in)
+    for s in range(behind + 1, last):
+        back_second(s)
     for s in range(SPLITS[2]):
         combine(0, s)
-    for s in range(last - 1):
+    for s in range(behind, last - 1):
+        back_last(s)
+    for s in range(behind):
         combine(1, s)
 
-    for q in range(2):
-        ref = x.at[q, pl.ds(0, 7)]
-        remote(ref, ref, ag_send.at[q], ag_recv.at[q, 0, 0], t, e).wait_send()
-        remote(ref, ref, rs_send.at[q], rs_recv.at[q, 0, 0], t, e).wait_send()
-    for n in range(4):
-        ref = slab[n].at[:, pl.ds(0, experts - 1)]
-        remote(ref, ref, a2a_send.at[n], a2a_recv.at[n, 0], t, e).wait_send()
-    combine(1, last - 1)
+    def sent(ref, sem):
+        remote(ref, ref, sem, ring_recv.at[0, 0], t, e).wait_send()
+
+    ahead = AHEAD * (dim // SPLITS[0])
+    sent(x.at[0, pl.ds(0, 7), :, :, pl.ds(ahead, dim - ahead)], ag_send.at[0])
+    sent(x.at[1, pl.ds(0, 7)], ag_send.at[1])
+    sent(x.at[0, pl.ds(0, 4), :, :, pl.ds(0, ahead)], mate_send)
+    sent(ring.at[:, pl.ds(0, 3)], ring_send)
+    sent(ringland.at[:, :, pl.ds(0, experts - 1)], spread_send)
+    wait_cols = behind * (dim // last)
+    sent(part.at[0, pl.ds(0, 7)], rs_send.at[0])
+    sent(part.at[1, pl.ds(0, 7), :, :, pl.ds(0, wait_cols)], rs_send.at[1])
+    sent(part.at[1, pl.ds(0, 4), :, :, pl.ds(wait_cols, dim - wait_cols)], backmate_send)
+    sent(backslab.at[:, :, pl.ds(0, experts - 1)], back_send)
+    sent(backslab.at[:, pl.ds(0, 3)], backring_send)
+    for n, (first, end) in enumerate(
+        ((AHEAD, SPLITS[0]), (0, SPLITS[1]), (0, SPLITS[2]), (0, behind))
+    ):
+        ref = slab[n].at[first:end, pl.ds(0, experts - 1)]
+        sent(ref, a2a_send.at[n])
+    back_last(last - 1)
 
 
 def store(*refs):
-    count = len(refs) // 2
-    sem = refs[-1]
     copies = [
-        pltpu.make_async_copy(a, b, sem.at[i])
-        for i, (a, b) in enumerate(zip(refs[:count], refs[count : 2 * count]))
+        pltpu.make_async_copy(a, b, refs[-1].at[i])
+        for i, (a, b) in enumerate(zip(refs[:4], refs[4:8]))
     ]
     for copy in copies:
         copy.start()
@@ -505,7 +735,6 @@
     shape = jax.ShapeDtypeStruct
     dma = pltpu.SemaphoreType.DMA
     shapes = (tokens.shape, tokens.shape, w_in.shape, w_down.shape)
-    most = max(SPLITS)
     boxes = [
         pltpu.VMEM((n, experts, group, dim // n // PIECES), BF16) for n in SPLITS
     ]
@@ -532,11 +761,27 @@
             pltpu.VMEM((2, PIECES * rows, experts * group), BF16),
             dma((6,)),
             dma((4,)),
-            dma((4, most)),
+            dma((sum(SPLITS),)),
             dma((2,)),
-            dma((2, max(SPLITS[:2]), 4)),
+            dma((sum(SPLITS[:2]), 4)),
             dma((2,)),
-            dma((2, max(SPLITS[2:]), 4)),
+            dma((sum(SPLITS[2:]), 4)),
+            pltpu.VMEM((AHEAD, 4) + boxes[0].shape[1:], BF16),
+            pltpu.VMEM((AHEAD, 4) + boxes[0].shape[1:], BF16),
+            dma(()),
+            dma((AHEAD, 3)),
+            dma(()),
+            dma((AHEAD, 4)),
+            dma(()),
+            pltpu.VMEM((BEHIND, 4) + boxes[3].shape[1:], BF16),
+            pltpu.VMEM((BEHIND, 4) + boxes[3].shape[1:], BF16),
+            pltpu.VMEM((BEHIND, 2, experts // 2) + boxes[3].shape[2:], BF16),
+            pltpu.VMEM((BEHIND, 2) + boxes[3].shape[1:], BF16),
+            dma(()),
+            dma((BEHIND, 4)),
+            dma(()),
+            dma((BEHIND, 2)),
+            dma(()),
         ]
         + boxes * 2,
         compiler_params=pltpu.CompilerParams(

time: 61.3 us -> 55.4 us (0.904)
  Pallas kernels: 60.5 us -> 54.5 us
    pallas_call x1, Pallas kernels: 58 us -> 51.9 us  [body(): pl.pallas_call(functools.partial(kernel, experts), out_shape=tuple((pltpu...]
where the time goes in v3:
time: 55.4 us; the launch traced here: 55.3 us
  Pallas kernels  54.5 us (98%)
  between operations  0.8 us (1%)
    pallas_call x1, Pallas kernels, body(): pl.pallas_call(functools.partial(kernel, experts), out_shape=tuple((pltpu...  51.9 us
    pallas_call x1, Pallas kernels, body(): pl.pallas_call(store, out_shape=tuple((shape(s, BF16) for s in shapes)),...  2.56 us

profile of v3, /device:TPU:0, one launch (start us, length us, event | category | flops | bytes accessed | tf_op | source)
XLA Modules:
  0.0 55.3 jit_solution(2051296218007237171)
XLA Ops:
  0.6 51.9 %shard_map.93 = (bf16[64,4096]{1,0:T(8,128)(2,1)S(1)}, bf16[64,4096]{1,0:T(8,128)(2,1)S(1)}, bf16[1,2,192,4096]{3,2,1,0:T(8,128)(2,1)S(1)}, bf16[1,192,4096]{2,1,0:T(8,128)(2,1)S(1)}) custom-call(s32[8,64]{1,0:T(8,128)} %bitcast.2, bf16[8,64]{1,0:T(8,128)(2,1)} %bitcast.3, bf16[64,4096]{1,0:T(8,128)(2,1)} %tok_hbm.1, bf16[64,4096]{1,0:T(8,128)(2,1)} %cot_hbm.1, ...), custom_call_target="tpu_custom_call" | custom-call | tf_op jit(solution)/shard_map/pallas_call | solution.py:741
  52.6 2.6 %shard_map.94 = (bf16[64,4096]{1,0:T(8,128)(2,1)}, bf16[64,4096]{1,0:T(8,128)(2,1)}, bf16[1,2,192,4096]{3,2,1,0:T(8,128)(2,1)}, bf16[1,192,4096]{2,1,0:T(8,128)(2,1)}) custom-call(bf16[64,4096]{1,0:T(8,128)(2,1)S(1)} %get-tuple-element.8.refs_0_, bf16[64,4096]{1,0:T(8,128)(2,1)S(1)} %get-tuple-element.9.refs_1_, ...), custom_call_target="tpu_custom_call" | custom-call | tf_op jit(solution)/shard_map/pallas_call | solution.py:791

commit v4 on v3

--- a/solution.py
+++ b/solution.py
@@ -13,6 +13,7 @@
 F32 = jnp.float32
 VMEM_LIMIT = 61_270_000
 AHEAD = 2
+CHUNKS = 4
 BEHIND = 2
 SPLITS = (4, 4, 4, 4)
 MESH = pl.DeviceIdType.MESH
@@ -34,8 +35,27 @@
     return lax.broadcasted_iota(jnp.int32, shape, dim)
 
 
-def stream(n, s):
-    return sum(SPLITS[:n]) + s
+def numbered(keys):
+    return {key: i for i, key in enumerate(keys)}
+
+
+A2A = numbered(
+    (n, s)
+    for n in range(4)
+    for s in range(AHEAD if n == 0 else 0, SPLITS[n] - (BEHIND if n == 3 else 0))
+)
+GATHER = numbered(
+    (q, s, kind)
+    for q in range(2)
+    for s in range(SPLITS[q])
+    for kind in range(3 if q == 0 and s < AHEAD else 0, 4)
+)
+REDUCE = numbered(
+    (q, s, kind)
+    for q in range(2)
+    for s in range(SPLITS[2 + q])
+    for kind in range(2 if q == 1 and s >= SPLITS[3] - BEHIND else 0, 4)
+)
 
 
 def kernel(
@@ -59,6 +79,7 @@
     act,
     hid,
     hid_rows,
+    pair_rows,
     part,
     mate,
     summed,
@@ -96,7 +117,8 @@
     slots = CAP * experts
     msg_rows = experts * group
     all_rows = 8 * slots
-    chunk = dim // 8
+    chunk = dim // CHUNKS
+    ff = win.shape[1]
 
     t = lax.axis_index("tok")
     e = lax.axis_index("exp")
@@ -208,7 +230,7 @@
                 slab[n].at[s, peer],
                 land[n].at[s, e],
                 a2a_send.at[n],
-                a2a_recv.at[stream(n, s)],
+                a2a_recv.at[A2A[n, s]],
                 t,
                 peer,
             )
@@ -220,7 +242,7 @@
 
     def exchanged(n, s):
         ref = land[n].at[s, pl.ds(0, experts - 1)]
-        remote(ref, ref, a2a_send.at[n], a2a_recv.at[stream(n, s)], t, e).wait_recv()
+        remote(ref, ref, a2a_send.at[n], a2a_recv.at[A2A[n, s]], t, e).wait_recv()
         return land[n][s].reshape(msg_rows, span(n, s)[1])
 
     def ring_copy(s, n):
@@ -283,7 +305,7 @@
         block = lax.rem(t + 2 * d, 8)
         put_rows(0, s, block, ringland[s, d])
         ref = x.at[0, block, :, :, span(0, s)[0]]
-        remote(ref, ref, mate_send, ag_recv.at[stream(0, s), 3], mate_t, e).start()
+        remote(ref, ref, mate_send, ag_recv.at[GATHER[0, s, 3]], mate_t, e).start()
 
     pick_table = table(picked)
     loads[2].wait()
@@ -344,11 +366,11 @@
             (opp, 1, mate_t),
         )[n]
         ref = ag_ref(q, s, block, half)
-        return remote(ref, ref, ag_send.at[q], ag_recv.at[stream(q, s), n % 3 if n < 6 else 3], dev, e)
+        return remote(ref, ref, ag_send.at[q], ag_recv.at[GATHER[q, s, n % 3 if n < 6 else 3]], dev, e)
 
     def ag_arrived(q, s, n):
         ref = x.at[q, pl.ds(0, 4 if n == 3 else 1), :, :, span(q, s)[0]]
-        remote(ref, ref, ag_send.at[q], ag_recv.at[stream(q, s), n], t, e).wait_recv()
+        remote(ref, ref, ag_send.at[q], ag_recv.at[GATHER[q, s, n]], t, e).wait_recv()
 
     def ag_first(q, s):
         for n in (0, 3, 1, 4, 6):
@@ -392,12 +414,12 @@
             )[n]
         kind = (0, 1, 1, 0, 1, 1, 2, 3, 3, 3)[n]
         sem = backmate_send if q == 1 and s >= behind else rs_send.at[q]
-        return remote(a, b, sem, rs_recv.at[stream(2 + q, s) - stream(2, 0), kind], dev, e)
+        return remote(a, b, sem, rs_recv.at[REDUCE[q, s, kind]], dev, e)
 
     def rs_arrived(q, s, kind):
         ref = (far.at[q], near.at[q], mate.at[q, 0], mate.at[q, pl.ds(0, 3)])[kind]
         ref = ref.at[..., span(2 + q, s)[0]]
-        remote(ref, ref, rs_send.at[q], rs_recv.at[stream(2 + q, s) - stream(2, 0), kind], t, e).wait_recv()
+        remote(ref, ref, rs_send.at[q], rs_recv.at[REDUCE[q, s, kind]], t, e).wait_recv()
 
     def rs_pair(q, s):
         for n in range(6, 10):
@@ -539,16 +561,16 @@
             lax.fori_loop(first, first + count, body, 0)
 
     def chunks(n, s, step):
-        count = 8 // SPLITS[n]
+        count = CHUNKS // SPLITS[n]
         over(s * count, count, step)
 
     def forward(cols):
         piece = x[0, :, :, :, cols].reshape(all_rows, chunk)
-        act[0] += dot_nt(win[0, :, cols], piece)
-        act[1] += dot_nt(win[1, :, cols], piece)
+        both = dot_nt(win[:, :, cols].reshape(2 * ff, chunk), piece)
+        act[0:2] += both.reshape(2, ff, all_rows)
 
     def terms_out(cols):
-        piece = dot(hid_rows[0], wdn[:, cols]).astype(BF16)
+        piece = dot(hid_rows[...], wdn[:, cols]).astype(BF16)
         part[0, :, :, :, cols] = piece.reshape(8, 2, experts, chunk)
 
     def backward(cols):
@@ -556,7 +578,7 @@
         act[2] += dot_nt(wdn[:, cols], piece)
 
     def terms_grad(cols):
-        piece = dot(hid_rows[1], win[0, :, cols]) + dot(hid_rows[2], win[1, :, cols])
+        piece = dot(pair_rows[...], win[:, :, cols].reshape(2 * ff, chunk))
         part[1, :, :, :, cols] = piece.astype(BF16).reshape(8, 2, experts, chunk)
 
     def weights_down(cols):
@@ -565,12 +587,15 @@
 
     def weights_in(cols):
         piece = x[0, :, :, :, cols].reshape(all_rows, chunk)
-        gin[0, 0, :, cols] = dot(hid[1], piece).astype(BF16)
-        gin[0, 1, :, cols] = dot(hid[2], piece).astype(BF16)
+        both = dot(hid[1:3].reshape(2 * ff, all_rows), piece).astype(BF16)
+        gin[0, :, :, cols] = both.reshape(2, ff, chunk)
 
     def keep(i, value):
         hid[i] = value.astype(BF16)
-        hid_rows[i] = value.T.astype(BF16)
+        if i == 0:
+            hid_rows[...] = value.T.astype(BF16)
+        else:
+            pair_rows[:, (i - 1) * ff : i * ff] = value.T.astype(BF16)
 
     act[...] = jnp.zeros_like(act)
     for s in range(AHEAD):
@@ -653,37 +678,34 @@
         if s >= 2 and s - 2 < behind:
             rs_far(1, s - 2)
     rs_second(0, 2)
+    rs_second(0, 3)
     for s in range(2, behind):
         rs_far(1, s)
     for s in range(min(2, behind)):
         rs_near(1, s)
     back_spread(2)
-    rs_second(0, 3)
     back_spread(1)
     back_spread(3)
-    over(0, 4, weights_down)
+    over(0, CHUNKS // 2, weights_down)
     for s in range(min(2, behind)):
         rs_second(1, s)
     back_spread(0)
     for s in range(2, behind):
         rs_near(1, s)
-    over(4, 4, weights_down)
-    back_far(behind)
-    over(0, 4, weights_in)
-    for s in range(behind + 1, last):
+    for s in range(behind, last):
         back_far(s)
     for s in range(SPLITS[2]):
         rs_last(0, s)
     for s in range(2, behind):
         rs_second(1, s)
+    over(CHUNKS // 2, CHUNKS // 2, weights_down)
+    for s in range(behind):
+        rs_last(1, s)
     for s in range(behind, last):
         back_near(s)
-    for s in range(behind):
-        rs_last(1, s)
-    back_second(behind)
-    over(4, 4, weights_in)
-    for s in range(behind + 1, last):
+    for s in range(behind, last):
         back_second(s)
+    over(0, CHUNKS, weights_in)
     for s in range(SPLITS[2]):
         combine(0, s)
     for s in range(behind, last - 1):
@@ -692,7 +714,7 @@
         combine(1, s)
 
     def sent(ref, sem):
-        remote(ref, ref, sem, ring_recv.at[0, 0], t, e).wait_send()
+        remote(ref, ref, sem, sem, t, e).wait_send()
 
     ahead = AHEAD * (dim // SPLITS[0])
     sent(x.at[0, pl.ds(0, 7), :, :, pl.ds(ahead, dim - ahead)], ag_send.at[0])
@@ -752,7 +774,8 @@
             pltpu.VMEM((2, 8, 2, experts, dim), BF16),
             pltpu.VMEM((3, ff, 16 * experts), F32),
             pltpu.VMEM((3, ff, 16 * experts), BF16),
-            pltpu.VMEM((3, 16 * experts, ff), BF16),
+            pltpu.VMEM((16 * experts, ff), BF16),
+            pltpu.VMEM((16 * experts, 2 * ff), BF16),
             pltpu.VMEM((2, 8, 2, experts, dim), BF16),
             pltpu.VMEM((2, 4, 2, experts, dim), BF16),
             pltpu.VMEM((2, 4, 2, experts, dim), BF16),
@@ -761,11 +784,11 @@
             pltpu.VMEM((2, PIECES * rows, experts * group), BF16),
             dma((6,)),
             dma((4,)),
-            dma((sum(SPLITS),)),
+            dma((len(A2A),)),
             dma((2,)),
-            dma((sum(SPLITS[:2]), 4)),
+            dma((len(GATHER),)),
             dma((2,)),
-            dma((sum(SPLITS[2:]), 4)),
+            dma((len(REDUCE),)),
             pltpu.VMEM((AHEAD, 4) + boxes[0].shape[1:], BF16),
             pltpu.VMEM((AHEAD, 4) + boxes[0].shape[1:], BF16),
             dma(()),

time: 55.4 us -> 54.2 us (0.978)
  Pallas kernels: 54.5 us -> 52.9 us
    pallas_call x1, Pallas kernels: 51.9 us -> 50.3 us  [body(): pl.pallas_call(functools.partial(kernel, experts), out_shape=tuple((pltpu...]
where the time goes in v4:
time: 54.2 us; the launch traced here: 53.7 us
  Pallas kernels  52.9 us (98%)
  between operations  0.8 us (1%)
    pallas_call x1, Pallas kernels, body(): pl.pallas_call(functools.partial(kernel, experts), out_shape=tuple((pltpu...  50.3 us
    pallas_call x1, Pallas kernels, body(): pl.pallas_call(store, out_shape=tuple((shape(s, BF16) for s in shapes)),...  2.56 us

profile of v4, /device:TPU:0, one launch (start us, length us, event | category | flops | bytes accessed | tf_op | source)
XLA Modules:
  0.0 53.7 jit_solution(11694993436454988546)
XLA Ops:
  0.6 50.3 %shard_map.93 = (bf16[64,4096]{1,0:T(8,128)(2,1)S(1)}, bf16[64,4096]{1,0:T(8,128)(2,1)S(1)}, bf16[1,2,192,4096]{3,2,1,0:T(8,128)(2,1)S(1)}, bf16[1,192,4096]{2,1,0:T(8,128)(2,1)S(1)}) custom-call(s32[8,64]{1,0:T(8,128)} %bitcast.2, bf16[8,64]{1,0:T(8,128)(2,1)} %bitcast.3, bf16[64,4096]{1,0:T(8,128)(2,1)} %tok_hbm.1, bf16[64,4096]{1,0:T(8,128)(2,1)} %cot_hbm.1, ...), custom_call_target="tpu_custom_call" | custom-call | tf_op jit(solution)/shard_map/pallas_call | solution.py:763
  51.0 2.6 %shard_map.94 = (bf16[64,4096]{1,0:T(8,128)(2,1)}, bf16[64,4096]{1,0:T(8,128)(2,1)}, bf16[1,2,192,4096]{3,2,1,0:T(8,128)(2,1)}, bf16[1,192,4096]{2,1,0:T(8,128)(2,1)}) custom-call(bf16[64,4096]{1,0:T(8,128)(2,1)S(1)} %get-tuple-element.8.refs_0_, bf16[64,4096]{1,0:T(8,128)(2,1)S(1)} %get-tuple-element.9.refs_1_, ...), custom_call_target="tpu_custom_call" | custom-call | tf_op jit(solution)/shard_map/pallas_call | solution.py:814

commit v5 on v4

--- a/solution.py
+++ b/solution.py
@@ -12,7 +12,7 @@
 BF16 = jnp.bfloat16
 F32 = jnp.float32
 VMEM_LIMIT = 61_270_000
-AHEAD = 2
+AHEAD = 3
 CHUNKS = 4
 BEHIND = 2
 SPLITS = (4, 4, 4, 4)
@@ -67,7 +67,8 @@
     win_hbm,
     wdn_hbm,
     moe,
-    tgr,
+    late,
+    placed,
     gin,
     gdn,
     ids_ref,
@@ -528,7 +529,7 @@
         own = backland[b, 0].astype(F32)
         back_ring_arrived(s, 1)
         total = own + backnear[b, 0].astype(F32) + backnear[b, 1].astype(F32)
-        put_out(1, s, total.astype(BF16).reshape(msg_rows, span(3, s)[1]))
+        late[s] = total.astype(BF16).reshape(msg_rows, span(3, s)[1])
 
     def rs_last(q, s):
         cols, width = span(2 + q, s)
@@ -538,17 +539,8 @@
         slab[2 + q][s] = as_message(total, width)
         exchange(2 + q, s)
 
-    def combine(q, s):
-        put_out(q, s, exchanged(2 + q, s))
-
-    def put_out(q, s, message):
-        start, width = span(2 + q, s)[0].start, span(2 + q, s)[1]
-        rows_out = dot(back[1 - q], message).astype(BF16)
-        out = (moe, tgr)[q]
-        for j in range(PIECES):
-            out[:, start + j * width : start + (j + 1) * width] = rows_out[
-                j * rows : (j + 1) * rows
-            ]
+    def combine(s):
+        put_back(moe, s, span(2, s), dot(back[...], exchanged(2, s)))
 
     def over(first, count, step):
         def body(k, carry):
@@ -619,8 +611,8 @@
         ring_take(s, 0)
     for s in later:
         ag_second(0, s)
-    back[0] = back_table(picked)
-    back[1] = back_table(weighted)
+    placed[...] = back_table(picked)
+    back[...] = back_table(weighted)
     for s in later:
         ag_third(0, s)
     for s in range(AHEAD):
@@ -707,11 +699,11 @@
         back_second(s)
     over(0, CHUNKS, weights_in)
     for s in range(SPLITS[2]):
-        combine(0, s)
+        combine(s)
     for s in range(behind, last - 1):
         back_last(s)
     for s in range(behind):
-        combine(1, s)
+        late[s] = exchanged(3, s)
 
     def sent(ref, sem):
         remote(ref, ref, sem, sem, t, e).wait_send()
@@ -736,13 +728,29 @@
     back_last(last - 1)
 
 
-def store(*refs):
+def put_back(out, s, cols, values):
+    start, width = cols[0].start, cols[1]
+    rows = out.shape[0]
+    values = values.astype(BF16)
+    for j in range(PIECES):
+        out[:, start + j * width : start + (j + 1) * width] = values[j * rows : (j + 1) * rows]
+
+
+def store(moe, late, placed, gin, gdn, moe_hbm, tgr_hbm, gin_hbm, gdn_hbm, tgr, sem):
     copies = [
-        pltpu.make_async_copy(a, b, refs[-1].at[i])
-        for i, (a, b) in enumerate(zip(refs[:4], refs[4:8]))
+        pltpu.make_async_copy(a, b, sem.at[i])
+        for i, (a, b) in enumerate(((gin, gin_hbm), (gdn, gdn_hbm), (moe, moe_hbm)))
     ]
     for copy in copies:
         copy.start()
+    count = late.shape[0]
+    size = tgr.shape[1] // count
+    for s in range(count):
+        cols = pl.ds(s * size, size)
+        put_back(tgr, s, (cols, size // PIECES), dot(placed[...], late[s]))
+        copy = pltpu.make_async_copy(tgr.at[:, cols], tgr_hbm.at[:, cols], sem.at[3 + s])
+        copy.start()
+        copies.append(copy)
     for copy in copies:
         copy.wait()
 
@@ -760,11 +768,18 @@
     boxes = [
         pltpu.VMEM((n, experts, group, dim // n // PIECES), BF16) for n in SPLITS
     ]
+    kept = (
+        tokens.shape,
+        (SPLITS[3], experts * group, dim // SPLITS[3] // PIECES),
+        (PIECES * rows, experts * group),
+        w_in.shape,
+        w_down.shape,
+    )
     results = pl.pallas_call(
         functools.partial(kernel, experts),
-        out_shape=tuple(pltpu.VMEM(s, BF16) for s in shapes),
+        out_shape=tuple(pltpu.VMEM(s, BF16) for s in kept),
         in_specs=[hbm] * 6,
-        out_specs=(vmem,) * 4,
+        out_specs=(vmem,) * 5,
         scratch_shapes=[
             pltpu.VMEM(expert_ids.shape[::-1], jnp.int32),
             pltpu.VMEM(expert_ids.shape[::-1], BF16),
@@ -781,7 +796,7 @@
             pltpu.VMEM((2, 4, 2, experts, dim), BF16),
             pltpu.VMEM((2, 2, experts, dim), BF16),
             pltpu.VMEM((2, 2, 2, experts, dim), BF16),
-            pltpu.VMEM((2, PIECES * rows, experts * group), BF16),
+            pltpu.VMEM((PIECES * rows, experts * group), BF16),
             dma((6,)),
             dma((4,)),
             dma((len(A2A),)),
@@ -814,10 +829,10 @@
     return pl.pallas_call(
         store,
         out_shape=tuple(shape(s, BF16) for s in shapes),
-        in_specs=[vmem] * 4,
+        in_specs=[vmem] * 5,
         out_specs=(hbm,) * 4,
-        scratch_shapes=[dma((4,))],
-        compiler_params=pltpu.CompilerParams(vmem_limit_bytes=1024 * 1024),
+        scratch_shapes=[pltpu.VMEM(tokens.shape, BF16), dma((3 + SPLITS[3],))],
+        compiler_params=pltpu.CompilerParams(vmem_limit_bytes=4 * 1024 * 1024),
     )(*results)
 
 

time: 54.2 us -> 52.8 us (0.974)
  Pallas kernels: 52.9 us -> 51.9 us
    pallas_call x1, Pallas kernels: 50.3 us -> 49.4 us  [body(): pl.pallas_call(functools.partial(kernel, experts), out_shape=tuple((pltpu...]
where the time goes in v5:
time: 52.8 us; the launch traced here: 52.7 us
  Pallas kernels  51.9 us (98%)
  between operations  0.8 us (2%)
    pallas_call x1, Pallas kernels, body(): pl.pallas_call(functools.partial(kernel, experts), out_shape=tuple((pltpu...  49.4 us
    pallas_call x1, Pallas kernels, body(): pl.pallas_call(store, out_shape=tuple((shape(s, BF16) for s in shapes)),...  2.55 us

profile of v5, /device:TPU:0, one launch (start us, length us, event | category | flops | bytes accessed | tf_op | source)
XLA Modules:
  0.0 52.7 jit_solution(10134480121809572855)
XLA Ops:
  0.6 49.4 %shard_map.93 = (bf16[64,4096]{1,0:T(8,128)(2,1)S(1)}, bf16[4,256,128]{2,1,0:T(8,128)(2,1)S(1)}, bf16[512,256]{1,0:T(8,128)(2,1)S(1)}, bf16[1,2,192,4096]{3,2,1,0:T(8,128)(2,1)S(1)}, bf16[1,192,4096]{2,1,0:T(8,128)(2,1)S(1)}) custom-call(s32[8,64]{1,0:T(8,128)} %bitcast.2, bf16[8,64]{1,0:T(8,128)(2,1)} %bitcast.3, bf16[64,4096]{1,0:T(8,128)(2,1)} %tok_hbm.1, ...), custom_call_target="tpu_custom_call" | custom-call | tf_op jit(solution)/shard_map/pallas_call | solution.py:778
  50.0 2.5 %shard_map.94 = (bf16[64,4096]{1,0:T(8,128)(2,1)}, bf16[64,4096]{1,0:T(8,128)(2,1)}, bf16[1,2,192,4096]{3,2,1,0:T(8,128)(2,1)}, bf16[1,192,4096]{2,1,0:T(8,128)(2,1)}) custom-call(bf16[64,4096]{1,0:T(8,128)(2,1)S(1)} %get-tuple-element.9.moe, bf16[4,256,128]{2,1,0:T(8,128)(2,1)S(1)} %get-tuple-element.10.late, ...), custom_call_target="tpu_custom_call" | custom-call | tf_op jit(solution)/shard_map/pallas_call | solution.py:829

commit v6 on v5

--- a/solution.py
+++ b/solution.py
@@ -613,11 +613,13 @@
         ag_second(0, s)
     placed[...] = back_table(picked)
     back[...] = back_table(weighted)
+    for s in range(AHEAD - 1):
+        ring_take(s, 1)
+        ring_take(s, 3)
     for s in later:
         ag_third(0, s)
-    for s in range(AHEAD):
-        ring_take(s, 1)
-        ring_take(s, 3)
+    ring_take(AHEAD - 1, 1)
+    ring_take(AHEAD - 1, 3)
     loads[4].wait()
     loads[5].wait()
     for s in later:
@@ -678,7 +680,6 @@
     back_spread(2)
     back_spread(1)
     back_spread(3)
-    over(0, CHUNKS // 2, weights_down)
     for s in range(min(2, behind)):
         rs_second(1, s)
     back_spread(0)
@@ -690,7 +691,7 @@
         rs_last(0, s)
     for s in range(2, behind):
         rs_second(1, s)
-    over(CHUNKS // 2, CHUNKS // 2, weights_down)
+    over(0, CHUNKS, weights_down)
     for s in range(behind):
         rs_last(1, s)
     for s in range(behind, last):

time: 52.8 us -> 52.7 us (level)
  no operation moved by 1% of the time
where the time goes in v6:
time: 52.7 us; the launch traced here: 52.6 us
  Pallas kernels  51.9 us (98%)
  between operations  0.64 us (1%)
    pallas_call x1, Pallas kernels, body(): pl.pallas_call(functools.partial(kernel, experts), out_shape=tuple((pltpu...  49.4 us
    pallas_call x1, Pallas kernels, body(): pl.pallas_call(store, out_shape=tuple((shape(s, BF16) for s in shapes)),...  2.55 us

profile of v6, /device:TPU:0, one launch (start us, length us, event | category | flops | bytes accessed | tf_op | source)
XLA Modules:
  0.0 52.6 jit_solution(3971420120035760146)
XLA Ops:
  0.6 49.4 %shard_map.93 = (bf16[64,4096]{1,0:T(8,128)(2,1)S(1)}, bf16[4,256,128]{2,1,0:T(8,128)(2,1)S(1)}, bf16[512,256]{1,0:T(8,128)(2,1)S(1)}, bf16[1,2,192,4096]{3,2,1,0:T(8,128)(2,1)S(1)}, bf16[1,192,4096]{2,1,0:T(8,128)(2,1)S(1)}) custom-call(s32[8,64]{1,0:T(8,128)} %bitcast.2, bf16[8,64]{1,0:T(8,128)(2,1)} %bitcast.3, bf16[64,4096]{1,0:T(8,128)(2,1)} %tok_hbm.1, ...), custom_call_target="tpu_custom_call" | custom-call | tf_op jit(solution)/shard_map/pallas_call | solution.py:779
  50.0 2.5 %shard_map.94 = (bf16[64,4096]{1,0:T(8,128)(2,1)}, bf16[64,4096]{1,0:T(8,128)(2,1)}, bf16[1,2,192,4096]{3,2,1,0:T(8,128)(2,1)}, bf16[1,192,4096]{2,1,0:T(8,128)(2,1)}) custom-call(bf16[64,4096]{1,0:T(8,128)(2,1)S(1)} %get-tuple-element.9.moe, bf16[4,256,128]{2,1,0:T(8,128)(2,1)S(1)} %get-tuple-element.10.late, ...), custom_call_target="tpu_custom_call" | custom-call | tf_op jit(solution)/shard_map/pallas_call | solution.py:830
